TPU v7x, 32 devices: a whole 2x2x4 slice. The times are simulated.
32 devices in a mesh: ctx: 8 (over y, x, core), fsdp: 4 (over z).
Axes of the slice: x: 2, y: 2, z: 4, core: 2. Of those that a mesh axis runs over, the one named last changes fastest.
Arguments:
- layer_input: bfloat16 [4, 1024, 960], P('fsdp', 'ctx'), may hold values from -60 to 60
- output_grad: bfloat16 [4, 1024, 960], P('fsdp', 'ctx'), may hold values from -6 to 6
- query_weight: bfloat16 [960, 960], P('fsdp'), may hold values from -0.1875 to 0.1875
- key_weight: bfloat16 [960, 320], P('fsdp'), may hold values from -0.1875 to 0.1875
- value_weight: bfloat16 [960, 320], P('fsdp'), may hold values from -0.1875 to 0.1875
- output_weight: bfloat16 [960, 960], P('fsdp'), may hold values from -6 to 6
- gate_weight: bfloat16 [960, 2560], P('fsdp'), may hold values from -0.1875 to 0.1875
- up_weight: bfloat16 [960, 2560], P('fsdp'), may hold values from -0.1875 to 0.1875
- down_weight: bfloat16 [2560, 960], P('fsdp'), may hold values from -0.125 to 0.125
- norm_gains: float32 [2, 960], replicated, may hold values from 0.5 to 1.5
- query_momentum: float32 [960, 960], P('fsdp'), may hold values from -160 to 160
- key_momentum: float32 [960, 320], P('fsdp'), may hold values from -384 to 384
- value_momentum: float32 [960, 320], P('fsdp'), may hold values from -384 to 384
- output_momentum: float32 [960, 960], P('fsdp'), may hold values from -40 to 40
- gate_momentum: float32 [960, 2560], P('fsdp'), may hold values from -80 to 80
- up_momentum: float32 [960, 2560], P('fsdp'), may hold values from -80 to 80
- down_momentum: float32 [2560, 960], P('fsdp'), may hold values from -80 to 80
- gain_momentum: float32 [2, 960], P(None, 'fsdp'), may hold values from -1024 to 1024
- block_order: int32 [16], replicated, may hold values from 0 to 15, each once
Outputs:
- layer_output: bfloat16 [4, 1024, 960], P('fsdp', 'ctx')
- input_gradient: float32 [4, 1024, 960], P('fsdp', 'ctx')
- query_gradient: float32 [960, 960], P('fsdp')
- key_gradient: float32 [960, 320], P('fsdp')
- value_gradient: float32 [960, 320], P('fsdp')
- output_gradient: float32 [960, 960], P('fsdp')
- gate_gradient: float32 [960, 2560], P('fsdp')
- up_gradient: float32 [960, 2560], P('fsdp')
- down_gradient: float32 [2560, 960], P('fsdp')
- gain_gradient: float32 [2, 960], P(None, 'fsdp')
- new_query_momentum: float32 [960, 960], P('fsdp')
- new_key_momentum: float32 [960, 320], P('fsdp')
- new_value_momentum: float32 [960, 320], P('fsdp')
- new_output_momentum: float32 [960, 960], P('fsdp')
- new_gate_momentum: float32 [960, 2560], P('fsdp')
- new_up_momentum: float32 [960, 2560], P('fsdp')
- new_down_momentum: float32 [2560, 960], P('fsdp')
- new_gain_momentum: float32 [2, 960], P(None, 'fsdp')
- new_query_weight: float32 [960, 960], P('fsdp')
- new_key_weight: float32 [960, 320], P('fsdp')
- new_value_weight: float32 [960, 320], P('fsdp')
- new_output_weight: float32 [960, 960], P('fsdp')
- new_gate_weight: float32 [960, 2560], P('fsdp')
- new_up_weight: float32 [960, 2560], P('fsdp')
- new_down_weight: float32 [2560, 960], P('fsdp')
- new_norm_gains: float32 [2, 960], P(None, 'fsdp')
Inputs may be any that keep to these rules, and one draw needn't show every extreme that they name: `block_order`: every block of a sequence stands in exactly one slot.
All inputs are finite; a program needn't handle non-finite values.
Results may differ from a plain program's by a relative error of at most 0.017.
Values may be sent and summed in bfloat16 or wider, within the bound.
A program may use at most 448 MiB of HBM per device.

v0:
```python
import functools
import math

import jax
import jax.numpy as jnp
from jax import lax
from jax.experimental import pallas as pl
from jax.experimental.pallas import tpu as pltpu
from jax.sharding import PartitionSpec as P

HEADS = 15
KV_HEADS = 5
HEAD = 64
NS_ITERS = 5


EPS = 1e-05
THETA = 100000.0
NS_A = 3.4445
NS_B = -4.775
NS_C = 2.0315
MOMENTUM = 0.95
RATE = 0.2
OUT_RATE = 6.0
GAIN_RATE = 0.002
MASKED = -1e30

MESH = pl.DeviceIdType.MESH
BF16 = jnp.bfloat16
F32 = jnp.float32
ANY = pl.BlockSpec(memory_space=pl.ANY)
VMEM = pl.BlockSpec(memory_space=pltpu.VMEM)
CLASSES = 8
WIDE = 6


def contract(left, right, left_dim, right_dim):
    return lax.dot_general(
        left, right, (((left_dim,), (right_dim,)), ((), ())), preferred_element_type=jnp.float32
    )


class Place:
    def __init__(self):
        self.parts = lax.axis_size("fsdp")
        self.extra = lax.axis_size("ctx") // CLASSES
        self.c = lax.axis_index("ctx")
        self.f = lax.axis_index("fsdp")
        self.p = lax.rem(self.c, CLASSES)
        self.core = lax.rem(self.c, 2)
        self.b1 = jnp.where(self.core == 0, 2, 4)
        self.b2 = jnp.where(self.core == 0, 4, 2)

    def peer(self, bits):
        return (self.c ^ bits, self.f)

    def along(self, j):
        return (self.c, self.f ^ j)

    def other(self, j):
        groups = self.extra
        return (lax.rem(self.c + CLASSES * j, CLASSES * groups), self.f)

    def barrier(self, bits=(1, 2, 4), line=True, others=False):
        sem = pltpu.get_barrier_semaphore()
        targets = [self.peer(b) for b in bits]
        if line:
            targets += [self.along(j) for j in range(1, self.parts)]
        if others:
            targets += [self.other(j) for j in range(1, self.extra)]
        for target in targets:
            pl.semaphore_signal(sem, inc=1, device_id=target, device_id_type=MESH)
        pl.semaphore_wait(sem, len(targets))


def remote(src, dst, send, recv, target):
    return pltpu.make_async_remote_copy(
        src_ref=src, dst_ref=dst, send_sem=send, recv_sem=recv, device_id=target, device_id_type=MESH
    )


def by_kind(cls, wide, tall):
    pl.when(cls < WIDE)(wide)
    pl.when(cls >= WIDE)(tall)


def weights_kernel(in_a, in_b, out_a, out_b, local, zs, s1, s2, sc, recv):
    at = Place()
    p, f, parts = at.p, at.f, at.parts
    at.barrier()
    copies = [
        pltpu.make_async_copy(in_a, out_a.at[:, f], local.at[0]),
        pltpu.make_async_copy(in_b, out_b.at[:, f], local.at[1]),
    ]
    for copy in copies:
        copy.start()

    def act(cls, j, g, send, target, what, first=False):
        def wide():
            dst = out_a.at[cls, g]
            src = in_a.at[cls] if first else dst
            getattr(remote(src, dst, send, recv.at[cls, j], target), what)()

        def tall():
            dst = out_b.at[cls - WIDE, g]
            src = in_b.at[cls - WIDE] if first else dst
            getattr(remote(src, dst, send, recv.at[cls, j], target), what)()

        by_kind(cls, wide, tall)

    sends = []

    def send(cls, j, g, sem, target, first=False):
        act(cls, j, g, sem, target, "start", first)
        sends.append((cls, j, g, sem, target, first))

    def arrived(cls, j):
        act(cls, j, f ^ j, zs.at[j], at.along(j), "wait_recv")

    for j in range(1, parts):
        send(p, j, f, zs.at[j], at.along(j), True)
    for j in range(1, parts):
        arrived(p, j)
        send(p, j, f ^ j, s1.at[0, j], at.peer(at.b1))
        send(p, j, f ^ j, s2.at[0, j], at.peer(at.b2))
        send(p, j, f ^ j, sc.at[0, j], at.peer(1))
    for j in range(1, parts):
        arrived(p ^ at.b1, j)
        send(p ^ at.b1, j, f ^ j, s2.at[1, j], at.peer(at.b2))
        send(p ^ at.b1, j, f ^ j, sc.at[1, j], at.peer(1))
    for slot, bits in ((2, at.b2), (3, at.b1 ^ at.b2)):
        for j in range(1, parts):
            arrived(p ^ bits, j)
            send(p ^ bits, j, f ^ j, sc.at[slot, j], at.peer(1))
    for bits in (1, 3, 5, 7):
        for j in range(1, parts):
            arrived(p ^ bits, j)
    for cls, j, g, sem, target, first in sends:
        act(cls, j, g, sem, target, "wait_send", first)
    for copy in copies:
        copy.wait()


def gather_weights(wide, tall):
    parts = lax.axis_size("fsdp")
    dma = pltpu.SemaphoreType.DMA
    return pl.pallas_call(
        weights_kernel,
        out_shape=(
            jax.ShapeDtypeStruct((WIDE, parts) + wide.shape[1:], BF16),
            jax.ShapeDtypeStruct((CLASSES - WIDE, parts) + tall.shape[1:], BF16),
        ),
        in_specs=[ANY, ANY],
        out_specs=(ANY, ANY),
        scratch_shapes=[
            dma((2,)),
            dma((parts,)),
            dma((1, parts)),
            dma((2, parts)),
            dma((4, parts)),
            dma((CLASSES, parts)),
        ],
        compiler_params=pltpu.CompilerParams(collective_id=0, has_side_effects=True),
        name="gather_weights",
    )(wide, tall)


def spread(at, own_a, own_b, out_a, out_b, local, ss, recv):
    p = at.p

    def act(cls, sem, target, what, first=False):
        def wide():
            dst = out_a.at[cls]
            getattr(remote(own_a if first else dst, dst, sem, recv.at[cls], target), what)()

        def tall():
            dst = out_b.at[cls - WIDE]
            getattr(remote(own_b if first else dst, dst, sem, recv.at[cls], target), what)()

        by_kind(cls, wide, tall)

    def keep(what):
        def wide():
            getattr(pltpu.make_async_copy(own_a, out_a.at[p], local), what)()

        def tall():
            getattr(pltpu.make_async_copy(own_b, out_b.at[p - WIDE], local), what)()

        by_kind(p, wide, tall)

    sends = []

    def send(cls, slot, target, first=False):
        act(cls, ss.at[slot], target, "start", first)
        sends.append((cls, slot, target, first))

    def arrived(cls):
        act(cls, ss.at[0], at.peer(1), "wait_recv")

    send(p, 0, at.peer(at.b1), True)
    send(p, 1, at.peer(at.b2), True)
    send(p, 2, at.peer(1), True)
    keep("start")

    def finish():
        arrived(p ^ at.b1)
        send(p ^ at.b1, 3, at.peer(at.b2))
        send(p ^ at.b1, 4, at.peer(1))
        arrived(p ^ at.b2)
        send(p ^ at.b2, 5, at.peer(1))
        arrived(p ^ at.b1 ^ at.b2)
        send(p ^ at.b1 ^ at.b2, 6, at.peer(1))
        for bits in (1, 3, 5, 7):
            arrived(p ^ bits)
        for cls, slot, target, first in sends:
            act(cls, ss.at[slot], target, "wait_send", first)
        keep("wait")

    return finish


def reduce_kernel(
    parts, extra, high,
    xt_in, dy_in, gain_in, m_qk, m_ov, m_gate, m_up, m_down,
    g_a, g_b, s_a, s_b, gain_out,
    xt, dy, p1s, p1r, p2s, p2r, own, own_t, za_s, za_r, zb_s, zb_r, ma, mb, ga, gb, sa, sb, es, er, gain_s, gain_r,
    ls, xs, xr, s1, r1, s2, r2, zs, zr, esem, ersem, msem, gs, gr, ag_l, ag_s, ag_r, ss, sr, sl,
):
    at = Place()
    p, f, core = at.p, at.f, at.core
    tokens = xt_in.shape[2]
    rows = ma.shape[0]
    half = dy.shape[2]

    def moment(what):
        for cls in range(CLASSES):
            @pl.when(p == cls)
            def _(cls=cls):
                side = cls % 2
                if cls < 2:
                    src, dst = (m_qk, m_ov)[cls], ma
                elif cls < WIDE:
                    whole = m_gate if cls < 4 else m_up
                    src, dst = whole.at[:, pl.ds(side * half, half)], ma
                else:
                    src, dst = m_down.at[pl.ds(side * high, high)], mb
                getattr(pltpu.make_async_copy(src, dst, msem), what)()

    moment("start")
    mine = [pltpu.make_async_copy(xt_in, xt.at[:, :, pl.ds(0, tokens)], ls.at[0])]
    for slot in range(4):
        mine.append(
            pltpu.make_async_copy(dy_in.at[core + 2 * slot], dy.at[slot, pl.ds(0, tokens)], ls.at[1 + slot])
        )
    mine.append(pltpu.make_async_copy(dy_in.at[8], dy.at[4, pl.ds(0, tokens)], ls.at[5]))
    for copy in mine:
        copy.start()
    at.barrier(others=True)
    pair = at.peer(1)
    theirs = [remote(xt_in, xt.at[:, :, pl.ds(tokens, tokens)], xs.at[0], xr.at[0], pair)]
    for slot in range(4):
        theirs.append(
            remote(dy_in.at[1 - core + 2 * slot], dy.at[slot, pl.ds(tokens, tokens)], xs.at[1 + slot], xr.at[1 + slot], pair)
        )
    theirs.append(remote(dy_in.at[8], dy.at[4, pl.ds(tokens, tokens)], xs.at[5], xr.at[5], pair))
    for copy in theirs:
        copy.start()

    def swap(slot, target):
        return remote(gain_s.at[slot], gain_r.at[slot], gs.at[slot], gr.at[slot], target)

    gain_s[0] = gain_in[...]
    swaps = [swap(0, pair)]
    swaps[0].start()
    for copy in mine:
        copy.wait()
    for copy in theirs:
        copy.wait()

    def term(cls, r):
        at_rows = pl.ds(pl.multiple_of(r * rows, rows), rows)
        slot = lax.div(cls, 2)
        kind = jnp.where(cls == 0, 0, jnp.where(cls == 1, 1, jnp.where(cls < WIDE, 2, 3)))
        value = jnp.dot(xt[kind, at_rows, :], dy[slot], preferred_element_type=F32)
        return value

    def with_values(cls, r, put):
        at_rows = pl.ds(pl.multiple_of(r * rows, rows), rows)

        @pl.when(cls == 1)
        def _():
            put(term(cls, r) + jnp.dot(xt[0, at_rows, :], dy[4], preferred_element_type=F32))

        @pl.when(cls != 1)
        def _():
            put(term(cls, r))

    def order(i):
        return lax.rem(f + 1 + i, parts)

    def one(slot, i):
        r = order(i)
        return remote(p1s.at[slot, r], p1r.at[slot, r], s1.at[slot, r], r1.at[slot, r], at.peer(at.b1))

    for slot, bits in ((0, at.b1 ^ at.b2), (1, at.b1)):
        def first(i, carry, slot=slot, bits=bits):
            r = order(i)

            def put(value):
                p1s[slot, r] = value.astype(BF16)

            with_values(p ^ bits, r, put)
            one(slot, i).start()
            return carry

        lax.fori_loop(0, parts, first, 0)

    swaps[0].wait()
    gain_s[1] = gain_s[0] + gain_r[0]
    swaps.append(swap(1, at.peer(2)))
    swaps[1].start()

    def two(i):
        r = order(i)
        return remote(p2s.at[r], p2r.at[r], s2.at[r], r2.at[r], at.peer(at.b2))

    def second(i, carry):
        r = order(i)
        one(0, i).wait_recv()

        def put(value):
            p2s[r] = (value + p1r[0, r].astype(F32)).astype(BF16)

        with_values(p ^ at.b2, r, put)
        two(i).start()
        return carry

    lax.fori_loop(0, parts, second, 0)
    swaps[1].wait()
    gain_s[2] = gain_s[1] + gain_r[1]
    swaps.append(swap(2, at.peer(4)))
    swaps[2].start()

    def line_a(r, source):
        return remote(za_s.at[r], za_r.at[source], zs.at[r], zr.at[source], (at.c, r))

    def line_b(r, source):
        return remote(
            zb_s.at[pl.ds(pl.multiple_of(r * high, high), high)],
            zb_r.at[source], zs.at[r], zr.at[source], (at.c, r),
        )

    early = extra == 1

    def third(i, carry):
        r = order(i)
        one(1, i).wait_recv()
        two(i).wait_recv()

        def put(value):
            total = value + p1r[1, r].astype(F32) + p2r[r].astype(F32)
            own[r] = total
            if early:
                za_s[r] = total.astype(BF16)

        with_values(p, r, put)
        if early:
            @pl.when((p < WIDE) & (i < parts - 1))
            def _():
                line_a(r, f).start()
        return carry

    lax.fori_loop(0, parts, third, 0)
    swaps[2].wait()
    gain_s[3] = gain_s[2] + gain_r[2]

    if not early:
        es[...] = own[...].astype(BF16)
        group = [
            remote(es, er.at[j - 1], esem.at[j - 1], ersem.at[j - 1], at.other(j)) for j in range(1, extra)
        ]
        for copy in group:
            copy.start()
        for j in range(1, extra):
            group[j - 1].wait_recv()
            own[...] = own[...] + er[j - 1].astype(F32)
        for copy in group:
            copy.wait_send()
        za_s[...] = own[...].astype(BF16)

        @pl.when(p < WIDE)
        def _():
            for j in range(1, parts):
                line_a(f ^ j, f).start()

    @pl.when(p >= WIDE)
    def _():
        for tile in range(half // 128):
            for r in range(parts):
                block = own[r, :, pl.ds(tile * 128, 128)]
                if rows % 128 == 0:
                    own_t[pl.ds(tile * 128, 128), pl.ds(r * rows, rows)] = block.T
            if rows % 128 != 0:
                column = own[:, :, pl.ds(tile * 128, 128)].reshape(parts * rows, 128)
                own_t[pl.ds(tile * 128, 128), :] = column.T
        zb_s[...] = own_t[...].astype(BF16)
        for j in range(1, parts):
            line_b(f ^ j, f).start()

    line_gain = [
        remote(gain_s.at[3], gain_r.at[3 + j], gs.at[3 + j], gr.at[3 + j], at.along(j)) for j in range(1, parts)
    ]
    other_gain = []
    for copy in line_gain:
        copy.start()

    moment("wait")

    @pl.when(p < WIDE)
    def _():
        total = own[f]
        for j in range(1, parts):
            line_a(f ^ j, f ^ j).wait_recv()
            total = total + za_r[f ^ j].astype(F32)
        ga[...] = total.astype(BF16)
        sa[...] = (MOMENTUM * ma[...] + total).astype(BF16)

    @pl.when(p >= WIDE)
    def _():
        total = own_t[pl.ds(pl.multiple_of(f * high, high), high), :]
        for j in range(1, parts):
            line_b(f ^ j, f ^ j).wait_recv()
            total = total + zb_r[f ^ j].astype(F32)
        gb[...] = total.astype(BF16)
        sb[...] = (MOMENTUM * mb[...] + total).astype(BF16)

    def share_a(j, source):
        return remote(sa, s_a.at[pl.ds(pl.multiple_of(source * rows, rows), rows)], ss.at[j], sr.at[j], at.along(j))

    def share_b(j, source):
        return remote(sb, s_b.at[pl.ds(pl.multiple_of(source * high, high), high)], ss.at[j], sr.at[j], at.along(j))

    @pl.when(p < WIDE)
    def _():
        for j in range(1, parts):
            share_a(j, f).start()
        pltpu.make_async_copy(sa, s_a.at[pl.ds(pl.multiple_of(f * rows, rows), rows)], sl).start()

    @pl.when(p >= WIDE)
    def _():
        for j in range(1, parts):
            share_b(j, f).start()
        pltpu.make_async_copy(sb, s_b.at[pl.ds(pl.multiple_of(f * high, high), high)], sl).start()

    finish = spread(at, ga, gb, g_a, g_b, ag_l, ag_s, ag_r)
    total = gain_s[3]
    for j in range(1, parts):
        line_gain[j - 1].wait()
        total = total + gain_r[3 + j]
    if extra > 1:
        gain_s[4] = total
        other_gain = [
            remote(gain_s.at[4], gain_r.at[3 + parts + j], gs.at[3 + parts + j], gr.at[3 + parts + j], at.other(j))
            for j in range(1, extra)
        ]
        for copy in other_gain:
            copy.start()
        for j in range(1, extra):
            other_gain[j - 1].wait()
            total = total + gain_r[3 + parts + j]
    gain_out[...] = total
    finish()

    for slot in range(2):
        lax.fori_loop(0, parts, lambda i, carry, slot=slot: (one(slot, i).wait_send(), carry)[1], 0)
    lax.fori_loop(0, parts, lambda i, carry: (two(i).wait_send(), carry)[1], 0)

    @pl.when(p < WIDE)
    def _():
        for j in range(1, parts):
            line_a(f ^ j, f).wait_send()
            share_a(j, f).wait_send()
            share_a(j, f ^ j).wait_recv()
        pltpu.make_async_copy(sa, s_a.at[pl.ds(pl.multiple_of(f * rows, rows), rows)], sl).wait()

    @pl.when(p >= WIDE)
    def _():
        for j in range(1, parts):
            line_b(f ^ j, f).wait_send()
            share_b(j, f).wait_send()
            share_b(j, f ^ j).wait_recv()
        pltpu.make_async_copy(sb, s_b.at[pl.ds(pl.multiple_of(f * high, high), high)], sl).wait()


def reduce_gradients(xt, dy, gains, moments, rows, high):
    parts = lax.axis_size("fsdp")
    extra = lax.axis_size("ctx") // CLASSES
    kinds, depth, tokens = xt.shape
    half = dy.shape[2]
    dma = pltpu.SemaphoreType.DMA
    vm = pltpu.VMEM
    n_gain = 4 + parts + extra
    group = max(extra - 1, 1)
    spare = (parts, rows, half) if extra > 1 else (1, 16, 128)
    return pl.pallas_call(
        functools.partial(reduce_kernel, parts, extra, high),
        out_shape=(
            jax.ShapeDtypeStruct((WIDE, rows, half), BF16),
            jax.ShapeDtypeStruct((CLASSES - WIDE, high, depth), BF16),
            jax.ShapeDtypeStruct((depth, half), BF16),
            jax.ShapeDtypeStruct((half, depth), BF16),
            jax.ShapeDtypeStruct(gains.shape, F32),
        ),
        in_specs=[ANY, ANY, VMEM] + [ANY] * 5,
        out_specs=(ANY, ANY, ANY, ANY, VMEM),
        scratch_shapes=[
            vm((kinds, depth, 2 * tokens), BF16),
            vm((5, 2 * tokens, half), BF16),
            vm((2, parts, rows, half), BF16),
            vm((2, parts, rows, half), BF16),
            vm((parts, rows, half), BF16),
            vm((parts, rows, half), BF16),
            vm((parts, rows, half), F32),
            vm((half, depth), F32),
            vm((parts, rows, half), BF16),
            vm((parts, rows, half), BF16),
            vm((half, depth), BF16),
            vm((parts, high, depth), BF16),
            vm((rows, half), F32),
            vm((high, depth), F32),
            vm((rows, half), BF16),
            vm((high, depth), BF16),
            vm((rows, half), BF16),
            vm((high, depth), BF16),
            vm(spare, BF16),
            vm((group,) + spare, BF16),
            vm((5,) + gains.shape, F32),
            vm((n_gain,) + gains.shape, F32),
            dma((6,)), dma((6,)), dma((6,)),
            dma((2, parts)), dma((2, parts)), dma((parts,)), dma((parts,)), dma((parts,)), dma((parts,)),
            dma((group,)), dma((group,)), dma, dma((n_gain,)), dma((n_gain,)),
            dma, dma((7,)), dma((CLASSES,)), dma((parts,)), dma((parts,)), dma,
        ],
        compiler_params=pltpu.CompilerParams(
            collective_id=1, has_side_effects=True, vmem_limit_bytes=62 << 20
        ),
        name="reduce_gradients",
    )(xt, dy, gains, *moments)


def rounded(value):
    return value.astype(BF16)


def poly_rows(g, row_start, count):
    block = g[pl.ds(row_start, count), :]
    return rounded(NS_B * block.astype(F32) + NS_C * jnp.dot(block, g[...], preferred_element_type=F32))


def ortho_kernel(
    parts, rows, high, narrow,
    s_a, s_b, o_a, o_b,
    x, x_t, gs, gr, g, poly, sq, sq_r, pa, pb, kt,
    gsem, rsem, qs, qr, ag_l, ag_s, ag_r,
):
    at = Place()
    p, f = at.p, at.f
    depth, half = x.shape
    step = depth // 4
    at.barrier(line=False)
    pair = at.peer(1)

    @pl.when(p < WIDE)
    def _():
        x[...] = s_a[...]

    @pl.when(p >= WIDE)
    def _():
        for tile in range(half // 128):
            x[:, pl.ds(tile * 128, 128)] = s_b[pl.ds(tile * 128, 128), :].T

    def scale_of(total):
        return 1.0 / (jnp.sqrt(total) + 1e-07)

    def normal(ref, inverse):
        ref[...] = rounded(ref[...].astype(F32) * inverse)

    def exchange(slot, r):
        chunk = pl.ds(r * step, step)
        return remote(gs.at[chunk], gr.at[slot, chunk], gsem.at[r], rsem.at[slot, r], pair)

    def fill_poly():
        for r in range(4):
            poly[pl.ds(r * step, step), :] = poly_rows(g, r * step, step)

    my_rows = pl.ds(pl.multiple_of(f * rows, rows), rows)
    my_high = pl.ds(pl.multiple_of(f * high, high), high)

    @pl.when(p >= 2)
    def _():
        wide = x[...].astype(F32)
        sq[...] = jnp.broadcast_to(jnp.sum(wide * wide), sq.shape)
        copy = remote(sq, sq_r, qs, qr, pair)
        copy.start()
        copy.wait()
        normal(x, scale_of(sq[...] + sq_r[...])[:1, :1])

        def grams(slot):
            for r in range(4):
                gs[pl.ds(r * step, step), :] = rounded(contract(x[pl.ds(r * step, step), :], x[...], 1, 1))
                exchange(slot, r).start()
            for r in range(4):
                chunk = pl.ds(r * step, step)
                exchange(slot, r).wait()
                g[chunk, :] = rounded(gs[chunk, :].astype(F32) + gr[slot, chunk, :].astype(F32))

        def iterate(it, carry):
            grams(lax.rem(it, 2))
            fill_poly()
            for tile in range(half // 256):
                block = pl.ds(tile * 256, 256)
                x[:, block] = rounded(
                    NS_A * x[:, block].astype(F32) + jnp.dot(poly[...], x[:, block], preferred_element_type=F32)
                )
            return carry

        lax.fori_loop(0, NS_ITERS - 1, iterate, 0)
        grams((NS_ITERS - 1) % 2)

        @pl.when(p < WIDE)
        def _():
            mine = poly_rows(g, pl.multiple_of(f * rows, rows), rows)
            pa[...] = rounded(NS_A * x[my_rows, :].astype(F32) + jnp.dot(mine, x[...], preferred_element_type=F32))

        @pl.when(p >= WIDE)
        def _():
            fill_poly()
            for tile in range(half // 128):
                x_t[pl.ds(tile * 128, 128), :] = x[:, pl.ds(tile * 128, 128)].T
            block = x_t[my_high, :]
            pb[...] = rounded(NS_A * block.astype(F32) + jnp.dot(block, poly[...], preferred_element_type=F32))

    @pl.when(p < 2)
    def _():
        kt[...] = x[:, narrow:].T
        inverse_k = scale_of(jnp.sum(jnp.square(kt[...].astype(F32))))
        normal(kt, inverse_k)
        wide = x[:, :narrow].astype(F32)
        x[:, :narrow] = rounded(wide * scale_of(jnp.sum(wide * wide)))

        def narrow_step(it, carry):
            gram = rounded(contract(kt[...], kt[...], 1, 1))
            turn = rounded(NS_B * gram.astype(F32) + NS_C * jnp.dot(gram, gram, preferred_element_type=F32))
            kt[...] = rounded(NS_A * kt[...].astype(F32) + jnp.dot(turn, kt[...], preferred_element_type=F32))
            return carry

        lax.fori_loop(0, NS_ITERS, narrow_step, 0)

        def gram_of():
            for r in range(4):
                chunk = pl.ds(r * step, step)
                g[chunk, :] = rounded(contract(x[chunk, :narrow], x[:, :narrow], 1, 1))

        def square_step(it, carry):
            gram_of()
            fill_poly()
            x[:, :narrow] = rounded(
                NS_A * x[:, :narrow].astype(F32) + jnp.dot(poly[...], x[:, :narrow], preferred_element_type=F32)
            )
            return carry

        lax.fori_loop(0, NS_ITERS - 1, square_step, 0)
        gram_of()
        mine = poly_rows(g, pl.multiple_of(f * rows, rows), rows)
        square = rounded(
            NS_A * x[my_rows, :narrow].astype(F32) + jnp.dot(mine, x[:, :narrow], preferred_element_type=F32)
        )
        x[:, narrow:] = kt[...].T
        pa[:, :narrow] = square
        pa[:, narrow:] = x[my_rows, narrow:]

    spread(at, pa, pb, o_a, o_b, ag_l, ag_s, ag_r)()


def orthogonalize(s_a, s_b, rows, high, narrow):
    parts = lax.axis_size("fsdp")
    depth, half = s_a.shape
    dma = pltpu.SemaphoreType.DMA
    vm = pltpu.VMEM
    return pl.pallas_call(
        functools.partial(ortho_kernel, parts, rows, high, narrow),
        out_shape=(
            jax.ShapeDtypeStruct((WIDE, rows, half), BF16),
            jax.ShapeDtypeStruct((CLASSES - WIDE, high, depth), BF16),
        ),
        in_specs=[VMEM, VMEM],
        out_specs=(ANY, ANY),
        scratch_shapes=[
            vm((depth, half), BF16),
            vm((half, depth), BF16),
            vm((depth, depth), BF16),
            vm((2, depth, depth), BF16),
            vm((depth, depth), BF16),
            vm((depth, depth), BF16),
            vm((8, 128), F32),
            vm((8, 128), F32),
            vm((rows, half), BF16),
            vm((high, depth), BF16),
            vm((half - narrow, depth), BF16),
            dma((4,)), dma((2, 4)), dma, dma, dma, dma((7,)), dma((CLASSES,)),
        ],
        compiler_params=pltpu.CompilerParams(
            collective_id=2, has_side_effects=True, vmem_limit_bytes=62 << 20
        ),
        name="orthogonalize",
    )(s_a, s_b)


class Weights:
    def __init__(self, at, sources, homes, zs, s1, s2, sc, recv):
        self.at, self.sources, self.homes = at, sources, homes
        self.zs, self.s1, self.s2, self.sc, self.recv = zs, s1, s2, sc, recv
        self.sends = []

    def act(self, group, q, j, plane, send, target, what, first=False):
        recv = self.recv.at[group, q, j]
        home, source = self.homes[group], self.sources[group]
        rows = home.shape[-2] // (1 if group == 3 else self.at.parts)
        unit = -(-rows // (16 * CLASSES)) * 16
        last = rows - (CLASSES - 1) * unit

        def piece(count):
            def go():
                start = pl.multiple_of(q * unit, 16)
                if group == 3:
                    columns = home.shape[1] // self.at.parts
                    dst = home.at[pl.ds(start, count), pl.ds(pl.multiple_of(plane * columns, 128), columns)]
                    src = source.at[pl.ds(start, count)]
                elif group == 0:
                    dst = home.at[:, pl.ds(pl.multiple_of(plane * rows + start, 16), count)]
                    src = dst
                else:
                    dst = home.at[pl.ds(pl.multiple_of(plane * rows + start, 16), count)]
                    src = source.at[pl.ds(start, count)]
                getattr(remote(src if first else dst, dst, send, recv, target), what)()

            return go

        pl.when(q < CLASSES - 1)(piece(unit))
        pl.when(q == CLASSES - 1)(piece(last))

    def send(self, group, q, j, plane, sem, target, first=False):
        self.act(group, q, j, plane, sem, target, "start", first)
        self.sends.append((group, q, j, plane, sem, target, "wait_send", first))

    def arrived(self, group, q, j):
        at = self.at
        self.act(group, q, j, at.f ^ j, self.zs.at[group, j], at.peer(1), "wait_recv")

    def along(self, group):
        at = self.at
        for j in range(1, at.parts):
            self.send(group, at.p, j, at.f, self.zs.at[group, j], at.along(j), True)

    def first(self, group):
        at = self.at
        for j in range(1, at.parts):
            self.arrived(group, at.p, j)
            self.send(group, at.p, j, at.f ^ j, self.s1.at[group, j], at.peer(at.b1))
            self.send(group, at.p, j, at.f ^ j, self.s2.at[group, 0, j], at.peer(at.b2))
            self.send(group, at.p, j, at.f ^ j, self.sc.at[group, 0, j], at.peer(1))

    def second(self, group):
        at = self.at
        q = at.p ^ at.b1
        for j in range(1, at.parts):
            self.arrived(group, q, j)
            self.send(group, q, j, at.f ^ j, self.s2.at[group, 1, j], at.peer(at.b2))
            self.send(group, q, j, at.f ^ j, self.sc.at[group, 1, j], at.peer(1))

    def third(self, group):
        at = self.at
        for slot, bits in ((2, at.b2), (3, at.b1 ^ at.b2)):
            for j in range(1, at.parts):
                self.arrived(group, at.p ^ bits, j)
                self.send(group, at.p ^ bits, j, at.f ^ j, self.sc.at[group, slot, j], at.peer(1))

    def ready(self, group):
        at = self.at
        for bits in (1, 3, 5, 7):
            for j in range(1, at.parts):
                self.arrived(group, at.p ^ bits, j)

    def finish(self):
        for item in self.sends:
            self.act(*item)


def spread_even(at, own, out, local, ss, recv):
    p = at.p

    def copy_of(cls, slot, target, first=False):
        return remote(own if first else out.at[cls], out.at[cls], ss.at[slot], recv.at[cls], target)

    keep = pltpu.make_async_copy(own, out.at[p], local)
    sends = []

    def send(cls, slot, target, first=False):
        copy = copy_of(cls, slot, target, first)
        copy.start()
        sends.append(copy)

    def arrived(cls):
        copy_of(cls, 0, at.peer(1)).wait_recv()

    send(p, 0, at.peer(at.b1), True)
    send(p, 1, at.peer(at.b2), True)
    send(p, 2, at.peer(1), True)
    keep.start()

    def pass_on():
        arrived(p ^ at.b1)
        send(p ^ at.b1, 3, at.peer(at.b2))
        send(p ^ at.b1, 4, at.peer(1))
        arrived(p ^ at.b2)
        send(p ^ at.b2, 5, at.peer(1))
        arrived(p ^ at.b1 ^ at.b2)
        send(p ^ at.b1 ^ at.b2, 6, at.peer(1))

    def finish():
        for bits in (1, 3, 5, 7):
            arrived(p ^ bits)
        for copy in sends:
            copy.wait_send()
        keep.wait()

    return pass_on, finish


def step_kernel(
    x_ref, up_ref, gains_ref, cos_ref, low_ref, high_ref, bias_ref, wq, wk, wo, wv, wg_in, wu_in, wd_in,
    m_q, m_k, m_o, m_v, m_gate, m_up, m_down,
    out_ref, grad_ref, g_out, o_out, gain_out,
    w01, wg, wu, wd, probs, kv, rot, dkv, c_send, c4r, c2r, c1r, att, gate, lifted,
    xt_in, dy_in, dv_in, xf_all, xa_all, yf_all, yv_all, za_r, ma, mq, mk, gain_s, gain_r, sq, sq_r,
    local, zs, s1, s2, sc, recv, kvs, kvr, ds, dr,
    ls, xs, xr, ps, pr, ys, yr, as_, ar, vs, vr, hs, hr, ozs, ozr, msem, gs, gr, ag_l, ag_s, ag_r, ls_l, ls_r, lr_l, lr_r,
    gsem, rsem, qs, qr, ex_s, ex_r, fx_s, fx_r, og_l, og_s, og_r, free,
):
    at = Place()
    p, f, core, parts = at.p, at.f, at.core, at.parts
    width, tokens = x_ref.shape
    half = w01.shape[2]
    keys = half - width
    group = HEADS // KV_HEADS
    scale = 1.0 / math.sqrt(HEAD)
    rows = width // parts
    columns = 2 * half // parts
    tall = width // 2
    pair = at.peer(1)
    my_rows = pl.ds(pl.multiple_of(f * rows, 16), rows)

    weights = Weights(at, (None, wg_in, wu_in, wd_in), (w01, wg, wu, wd), zs, s1, s2, sc, recv)
    keep = [
        pltpu.make_async_copy(wg_in, wg.at[my_rows], local.at[0]),
        pltpu.make_async_copy(wu_in, wu.at[my_rows], local.at[1]),
        pltpu.make_async_copy(
            wd_in, wd.at[:, pl.ds(pl.multiple_of(f * columns, 128), columns)], local.at[2]
        ),
    ]

    def moment(what):
        for cls in range(CLASSES):
            @pl.when(p == cls)
            def _(cls=cls):
                side = cls % 2
                if cls < 2:
                    pairs = [((m_q, m_o)[cls], mq, 0), ((m_k, m_v)[cls], mk, 1)]
                elif cls < WIDE:
                    whole = m_gate if cls < 4 else m_up
                    pairs = [(whole.at[:, pl.ds(side * half, half)], ma, 0)]
                else:
                    pairs = [
                        (
                            m_down.at[pl.ds(side * tall + t * rows, rows)],
                            ma.at[:, pl.ds(t * columns, columns)],
                            t,
                        )
                        for t in range(2)
                    ]
                for src, dst, index in pairs:
                    getattr(pltpu.make_async_copy(src, dst, msem.at[index]), what)()

    w01[0, my_rows, :width] = wq[...]
    w01[0, my_rows, width:] = wk[...].T
    w01[1, my_rows, :width] = wo[...]
    w01[1, my_rows, width:] = wv[...].T
    at.barrier(bits=range(1, CLASSES))
    for index in range(4):
        weights.along(index)
    for copy in keep:
        copy.start()
    moment("start")

    residual = x_ref[...].astype(F32).T
    upstream = up_ref[...].astype(F32).T
    inverse_first = lax.rsqrt(jnp.mean(residual * residual, axis=-1, keepdims=True) + EPS)
    normed_first = (residual * inverse_first * gains_ref[0:1, :]).astype(BF16)
    xt_in[0] = normed_first.T
    xt_in[3] = up_ref[...]

    weights.first(0)
    weights.second(0)
    weights.first(1)
    weights.third(0)
    weights.ready(0)

    def turn(value, sign):
        tiles = []
        for tile in range(half // 128):
            part = value[:, tile * 128 : (tile + 1) * 128]
            swapped = pltpu.roll(part, HEAD // 2, 1) * low_ref[...] + pltpu.roll(part, 128 - HEAD // 2, 1) * high_ref[...]
            tiles.append(part * cos_ref[...] + swapped if sign > 0 else part * cos_ref[...] - swapped)
        return tiles

    qk = jnp.dot(normed_first, w01[0], preferred_element_type=F32)
    for tile, value in enumerate(turn(qk, 1)):
        rot[:, tile * 128 : (tile + 1) * 128] = value.astype(BF16)
    values = jnp.dot(normed_first, w01[1, :, width:], preferred_element_type=F32).astype(BF16)
    kv[p, :, :keys] = rot[:, width:]
    kv[p, :, keys:] = values

    def block(q, slot, target):
        return remote(kv.at[q], kv.at[q], kvs.at[slot], kvr.at[q], target)

    sent = [block(p, 0, at.peer(at.b1)), block(p, 1, at.peer(at.b2)), block(p, 2, at.peer(1))]
    for copy in sent:
        copy.start()

    def pass_keys(q, slots):
        block(q, 0, at.peer(1)).wait_recv()
        for slot, target in slots:
            copy = block(q, slot, target)
            copy.start()
            sent.append(copy)

    weights.second(1)
    pass_keys(p ^ at.b1, [(3, at.peer(at.b2)), (4, at.peer(1))])
    pass_keys(p ^ at.b2, [(5, at.peer(1))])
    weights.first(2)
    pass_keys(p ^ at.b1 ^ at.b2, [(6, at.peer(1))])
    for bits in (1, 3, 5, 7):
        pass_keys(p ^ bits, [])
    weights.third(1)

    def keys_of(g):
        return kv[:, :, g * HEAD : (g + 1) * HEAD].reshape(CLASSES * tokens, HEAD)

    def values_of(g):
        return kv[:, :, keys + g * HEAD : keys + (g + 1) * HEAD].reshape(CLASSES * tokens, HEAD)

    def heads_of(ref, g):
        return jnp.concatenate([ref[:, h * HEAD : (h + 1) * HEAD] for h in range(g * group, (g + 1) * group)], axis=0)

    def attend(g):
        scores = contract(keys_of(g), heads_of(rot, g), 1, 1) * scale
        bias = bias_ref[...].astype(F32)
        scores = scores + jnp.concatenate([bias] * group, axis=1)
        top = jnp.max(scores, axis=0, keepdims=True)
        expo = jnp.exp(scores - top)
        total = jnp.sum(expo, axis=0, keepdims=True)
        chance = expo * (1.0 / total)
        probs[g] = chance
        mixed = contract(values_of(g), chance.astype(BF16), 0, 0)
        turned = mixed.T.astype(BF16)
        for h in range(group):
            at_lane = (g * group + h) * HEAD
            att[:, at_lane : at_lane + HEAD] = turned[h * tokens : (h + 1) * tokens]

    attend(0)
    attend(1)
    weights.second(2)
    attend(2)
    weights.first(3)
    attend(3)
    weights.third(2)
    attend(4)
    for copy in keep:
        copy.wait()
    weights.ready(1)

    xt_in[1] = att[...].T
    middle = residual + jnp.dot(att[...], w01[1, :, :width], preferred_element_type=F32)
    inverse_second = lax.rsqrt(jnp.mean(middle * middle, axis=-1, keepdims=True) + EPS)
    normed_second = (middle * inverse_second * gains_ref[1:2, :]).astype(BF16)
    xt_in[2] = normed_second.T
    weights.second(3)
    gate[...] = jnp.dot(normed_second, wg[...], preferred_element_type=F32)
    weights.third(3)

    def tokens_of(q):
        return pl.ds(pl.multiple_of(q * tokens, tokens), tokens)

    def kind_of(q):
        return jnp.where(q < 2, 0, jnp.where(q < WIDE, 2, 3))

    own_x = pltpu.make_async_copy(xt_in.at[kind_of(p)], xf_all.at[:, tokens_of(p)], ls.at[0])

    def x_move(bits):
        q = p ^ bits
        return remote(xt_in.at[kind_of(q)], xf_all.at[:, tokens_of(p)], xs.at[bits], xr.at[p], at.peer(bits))

    def a_move():
        return remote(xt_in.at[1], xa_all.at[:, tokens_of(p)], as_, ar.at[p], at.peer(p ^ 1))

    def own_a():
        return pltpu.make_async_copy(xt_in.at[1], xa_all.at[:, tokens_of(p)], ls.at[1])

    def y_move(bits):
        q = p ^ bits
        return remote(dy_in.at[q], yf_all.at[tokens_of(p)], ys.at[bits], yr.at[p], at.peer(bits))

    def own_y():
        return pltpu.make_async_copy(dy_in.at[p], yf_all.at[tokens_of(p)], ls.at[2])

    def v_move():
        return remote(dv_in, yv_all.at[tokens_of(p)], vs, vr.at[p], at.peer(p ^ 1))

    def own_v():
        return pltpu.make_async_copy(dv_in, yv_all.at[tokens_of(p)], ls.at[3])

    own_x.start()
    for bits in (2, 4, 6):
        x_move(bits).start()
    pl.when(p != 1)(lambda: a_move().start())
    pl.when(p == 1)(lambda: own_a().start())

    def give_y(bits, low, high):
        q = p ^ bits

        @pl.when((q >= low) & (q < high))
        def _():
            y_move(bits).start()

    weights.ready(2)
    for side in range(2):
        lifted[side * tokens : (side + 1) * tokens] = jnp.dot(
            normed_second, wu[:, side * half : (side + 1) * half], preferred_element_type=F32
        )

    def lift():
        return jnp.concatenate([lifted[:tokens], lifted[tokens:]], axis=1)

    hidden = (gate[...] * jax.nn.sigmoid(gate[...]) * lift()).astype(BF16)
    dy_in[6] = hidden[:, :half]
    dy_in[7] = hidden[:, half:]
    for bits in range(1, CLASSES):
        give_y(bits, WIDE, CLASSES)
    weights.ready(3)

    grad_hidden = jnp.dot(upstream.astype(BF16), wd[...], preferred_element_type=F32)
    sigma = jax.nn.sigmoid(gate[...])
    grad_gate = (grad_hidden * lift() * sigma * (1.0 + gate[...] * (1.0 - sigma))).astype(BF16)
    grad_lifted = (grad_hidden * gate[...] * sigma).astype(BF16)
    for side in range(2):
        lanes = slice(side * half, (side + 1) * half)
        dy_in[2 + side] = grad_gate[:, lanes]
        dy_in[4 + side] = grad_lifted[:, lanes]
    for bits in (1, at.b1, at.b1 ^ 1, at.b2, at.b2 ^ 1):
        give_y(bits, 2, WIDE)

    out_ref[...] = (middle + contract(hidden, wd[...], 1, 1)).T.astype(BF16)
    weights.finish()
    grad_normed = contract(grad_gate, wg[...], 1, 1) + contract(grad_lifted, wu[...], 1, 1)
    pl.semaphore_signal(free.at[0], inc=1, device_id=pair, device_id_type=MESH)

    def norm_back(value, inverse, gain, incoming):
        scaled = incoming * gain
        mean = jnp.mean(scaled * value, axis=-1, keepdims=True)
        through = inverse * scaled - value * (inverse * inverse * inverse) * mean
        return through, jnp.sum(incoming * value * inverse, axis=0, keepdims=True)

    through, gain_second = norm_back(middle, inverse_second, gains_ref[1:2, :], grad_normed)
    gain_s[0] = jnp.zeros(gain_s.shape[1:], F32)
    gain_s[0, 1:2, :] = gain_second
    grad_middle = upstream + through
    grad_branch = grad_middle.astype(BF16)
    dy_in[1, :, :width] = grad_branch
    dy_in[1, :, width:] = jnp.zeros((tokens, keys), BF16)
    att[...] = contract(grad_branch, w01[1, :, :width], 1, 1).astype(BF16)

    for bits in (1, at.b1, at.b1 ^ 1, at.b2, at.b2 ^ 1):
        give_y(bits, 1, 2)

    own = lifted.at[pl.ds(0, rows)]

    def swap(slot, target):
        return remote(gain_s.at[slot], gain_r.at[slot], gs.at[slot], gr.at[slot], target)

    def order(i):
        return lax.rem(f + 1 + i, parts)

    def room(r):
        return wd.at[pl.ds(pl.multiple_of(r * rows, 16), rows), pl.ds(half, half)]

    def line(r, source):
        return remote(room(r), za_r.at[(r ^ source) - 1], ozs.at[r], ozr.at[source], (at.c, r))

    def arrival(j):
        return remote(room(f), za_r.at[j - 1], ozs.at[f], ozr.at[f ^ j], at.along(j))

    middle_token = CLASSES // 2 * tokens

    def sides_of():
        return [
            remote(
                yf_all.at[pl.ds(side * middle_token, middle_token)],
                wu.at[pl.ds(0, middle_token), pl.ds(side * half, half)],
                hs.at[side], hr.at[side], pair,
            )
            for side in range(2)
        ]

    def produce(r, put):
        at_rows = pl.ds(pl.multiple_of(r * rows, 16), rows)
        every = slice(0, half)

        @pl.when(p == 1)
        def _():
            value = jnp.dot(xf_all[at_rows, :], yv_all[...], preferred_element_type=F32)
            put(slice(0, width), jnp.dot(xa_all[at_rows, :], yf_all[:, pl.ds(0, width)], preferred_element_type=F32))
            put(slice(width, half), value[:, :keys])

        @pl.when((p != 1) & (p < WIDE))
        def _():
            put(every, jnp.dot(xf_all[at_rows, :], yf_all[...], preferred_element_type=F32))

        @pl.when(p >= WIDE)
        def _():
            side, start = lax.div(r * columns, half), pl.multiple_of(lax.rem(r * columns, half), 128)
            for t in range(2):
                part_rows = pl.ds(pl.multiple_of((p - WIDE) * tall + t * rows, 16), rows)
                lanes = slice(t * columns, (t + 1) * columns)

                @pl.when(side == core)
                def _():
                    put(
                        lanes,
                        jnp.dot(xf_all[part_rows, :], yf_all[:, pl.ds(start, columns)], preferred_element_type=F32),
                    )

                @pl.when(side != core)
                def _():
                    put(
                        lanes,
                        jnp.dot(
                            xf_all[part_rows, pl.ds(0, middle_token)],
                            wu[pl.ds(0, middle_token), pl.ds(start, columns)],
                            preferred_element_type=F32,
                        )
                        + jnp.dot(
                            xf_all[part_rows, pl.ds(middle_token, middle_token)],
                            wu[pl.ds(0, middle_token), pl.ds(pl.multiple_of(half + start, 128), columns)],
                            preferred_element_type=F32,
                        ),
                    )

    def gradients():
        for bits in range(1, CLASSES):
            arrived_y(p ^ bits)

        @pl.when(p >= WIDE)
        def _():
            pl.semaphore_wait(free.at[0], 1)
            for copy in sides_of():
                copy.start()
            for copy in sides_of():
                copy.wait()

        @pl.when(p < WIDE)
        def _():
            pl.semaphore_wait(free.at[0], 1)

        def step_of(i, carry):
            r = order(i)

            def put(lanes, value):
                own[:, lanes] = value
                room(r)[:, lanes] = value.astype(BF16)

            produce(r, put)

            @pl.when(i < parts - 1)
            def _():
                line(r, f).start()

            return carry

        lax.fori_loop(0, parts, step_of, 0)

    def arrived_y(q):
        remote(dy_in.at[0], yf_all.at[tokens_of(q)], ys.at[1], yr.at[q], pair).wait_recv()

    def arrived_x(q):
        remote(xt_in.at[0], xf_all.at[:, tokens_of(q)], xs.at[2], xr.at[q], pair).wait_recv()

    def x_pair(bits):
        q = p ^ bits
        return remote(xf_all.at[:, tokens_of(q)], xf_all.at[:, tokens_of(q)], ps.at[bits], pr.at[q], pair)

    def attend_back(g):
        chance = probs[g]
        out_grad = heads_of(att, g)
        query = heads_of(rot, g)
        grad_probs = contract(values_of(g), out_grad, 1, 1)
        delta = jnp.sum(grad_probs * chance, axis=0, keepdims=True)
        grad_scores = (chance * (grad_probs - delta)).astype(BF16)
        grad_values = jnp.dot(chance.astype(BF16), out_grad, preferred_element_type=F32)
        grad_keys = jnp.dot(grad_scores, query, preferred_element_type=F32) * scale
        dkv[:, :, g * HEAD : (g + 1) * HEAD] = grad_keys.reshape(CLASSES, tokens, HEAD)
        dkv[:, :, keys + g * HEAD : keys + (g + 1) * HEAD] = grad_values.reshape(CLASSES, tokens, HEAD)
        turned = contract(keys_of(g), grad_scores, 0, 0).T * scale
        for h in range(group):
            at_lane = (g * group + h) * HEAD
            gate[:, at_lane : at_lane + HEAD] = turned[h * tokens : (h + 1) * tokens]

    for g in range(KV_HEADS):
        attend_back(g)

    def halve(bit, rest, sbuf, rbuf, index, between=None):
        for i, bits in enumerate(rest):
            sbuf[i // 2, :, pl.ds(i % 2 * 2 * keys, 2 * keys)] = dkv[p ^ bit ^ bits].astype(BF16)
        copy = remote(sbuf, rbuf, ds.at[index], dr.at[index], at.peer(bit))
        copy.start()
        if between is not None:
            between()
        copy.wait()
        for i, bits in enumerate(rest):
            dkv[p ^ bits] = dkv[p ^ bits] + rbuf[i // 2, :, pl.ds(i % 2 * 2 * keys, 2 * keys)].astype(F32)

    def diagonal():
        for bits in (at.b1 ^ at.b2, at.b1 ^ at.b2 ^ 1):
            give_y(bits, 1, WIDE)

    halve(1, (0, 2, 4, 6), c_send, c4r, 0)
    halve(at.b1, (0, at.b2), c4r.at[pl.ds(0, 1)], c2r, 1)
    halve(at.b2, (0,), c4r.at[pl.ds(1, 1), :, pl.ds(0, 2 * keys)], c1r, 2, diagonal)

    gate[:, width:half] = dkv[p, :, :keys]
    for tile, value in enumerate(turn(gate[:, :half], -1)):
        dy_in[0, :, tile * 128 : (tile + 1) * 128] = value.astype(BF16)
    dv_in[...] = jnp.zeros(dv_in.shape, BF16)
    dv_in[:, :keys] = dkv[p, :, keys:].astype(BF16)
    for bits in range(1, CLASSES):
        give_y(bits, 0, 1)
    pl.when(p != 1)(lambda: v_move().start())
    pl.when(p == 1)(lambda: own_v().start())
    own_y().start()

    own_x.wait()
    for bits in (2, 4, 6):
        arrived_x(p ^ bits)
    for bits in (0, 2, 4, 6):
        x_pair(bits).start()

    grad_normed = contract(dy_in[0], w01[0], 1, 1)
    grad_normed = grad_normed + contract(dv_in[:, :keys], w01[1, :, width:], 1, 1)
    through, gain_first = norm_back(residual, inverse_first, gains_ref[0:1, :], grad_normed)
    gain_s[0, 0:1, :] = gain_first
    swaps = [swap(0, pair)]
    swaps[0].start()
    grad_ref[...] = (grad_middle + through).T
    own_y().wait()
    for bits in (0, 2, 4, 6):
        x_pair(bits).wait_send()
        remote(
            xf_all.at[:, tokens_of(p ^ bits ^ 1)], xf_all.at[:, tokens_of(p ^ bits ^ 1)],
            ps.at[bits], pr.at[p ^ bits ^ 1], pair,
        ).wait_recv()

    @pl.when(p == 1)
    def _():
        own_a().wait()
        own_v().wait()
        for q in range(CLASSES):
            if q != 1:
                remote(xt_in.at[1], xa_all.at[:, tokens_of(q)], as_, ar.at[q], pair).wait_recv()
                remote(dv_in, yv_all.at[tokens_of(q)], vs, vr.at[q], pair).wait_recv()

    gradients()
    swaps[0].wait()
    gain_s[1] = gain_s[0] + gain_r[0]
    swaps.append(swap(1, at.peer(2)))
    swaps[1].start()
    for bits in range(1, CLASSES):
        y_move(bits).wait_send()
    for bits in (2, 4, 6):
        x_move(bits).wait_send()

    @pl.when(p != 1)
    def _():
        a_move().wait_send()
        v_move().wait_send()

    swaps[1].wait()
    gain_s[2] = gain_s[1] + gain_r[1]
    swaps.append(swap(2, at.peer(4)))
    swaps[2].start()

    moment("wait")

    @pl.when(p < 2)
    def _():
        ma[:, :width] = mq[...]
        ma[:, width:] = mk[...].T

    sall = wd.at[:, pl.ds(0, half)]
    ga, pa = (w01.at[1, pl.ds((parts - 1 - i) * rows, rows)] for i in range(2))
    total = own[...]
    for j in range(1, parts):
        arrival(j).wait_recv()
        total = total + za_r[j - 1].astype(F32)
    ga[...] = total.astype(BF16)
    sall[my_rows, :] = (MOMENTUM * ma[...] + total).astype(BF16)

    def shard(index):
        return sall.at[pl.ds(pl.multiple_of(index * rows, 16), rows)]

    def rightward(index):
        return remote(shard(index), shard(index), ls_r.at[index], lr_r.at[index], (at.c, lax.rem(f + 1, parts)))

    def leftward(index):
        return remote(shard(index), shard(index), ls_l.at[index], lr_l.at[index], (at.c, lax.rem(f + parts - 1, parts)))

    def can_right():
        return f < parts - 1

    def can_left():
        return f > 0

    pl.when(can_right())(lambda: rightward(f).start())
    pl.when(can_left())(lambda: leftward(f).start())

    pass_on, finish = spread_even(at, ga, g_out, ag_l, ag_s, ag_r)
    swaps[2].wait()
    gain_s[3] = gain_s[2] + gain_r[2]
    line_gain = [
        remote(gain_s.at[3], gain_r.at[3 + j], gs.at[3 + j], gr.at[3 + j], at.along(j)) for j in range(1, parts)
    ]
    for copy in line_gain:
        copy.start()

    for hop in range(1, parts):
        @pl.when(f - hop >= 0)
        def _(hop=hop):
            rightward(f - hop).wait_recv()
            pl.when(can_right())(lambda: rightward(f - hop).start())

        @pl.when(f + hop < parts)
        def _(hop=hop):
            leftward(f + hop).wait_recv()
            pl.when(can_left())(lambda: leftward(f + hop).start())

    pass_on()

    for j in range(1, parts):
        line(f ^ j, f).wait_send()
    pl.when(can_right())(lambda: rightward(f).wait_send())
    pl.when(can_left())(lambda: leftward(f).wait_send())
    for hop in range(1, parts):
        pl.when((f - hop >= 0) & can_right())(lambda hop=hop: rightward(f - hop).wait_send())
        pl.when((f + hop < parts) & can_left())(lambda hop=hop: leftward(f + hop).wait_send())
    pl.semaphore_signal(free.at[1], inc=1, device_id=pair, device_id_type=MESH)
    pl.semaphore_wait(free.at[1], 1)

    x = w01.at[0]
    wide_gram = 1024
    gram_s, g = wg.at[:, pl.ds(0, wide_gram)], wg.at[:, pl.ds(wide_gram, wide_gram)]
    poly, xf = wd.at[:, pl.ds(0, wide_gram)], wd.at[:, pl.ds(half, columns)]
    step = width // 4

    def gram_r(slot):
        return wu.at[:, pl.ds(slot * wide_gram, wide_gram)]

    def scale_of(total):
        return 1.0 / (jnp.sqrt(total) + 1e-07)

    def normal(ref, inverse):
        ref[...] = rounded(ref[...].astype(F32) * inverse)

    def exchange(slot, r):
        part = pl.ds(r * step, step)
        return remote(gram_s.at[part], gram_r(slot).at[part], gsem.at[r], rsem.at[slot, r], pair)

    def poly_of(start, count):
        part = g[pl.ds(start, count), pl.ds(0, width)]
        square = jnp.dot(part, g[:, pl.ds(0, width)], preferred_element_type=F32)
        return rounded(NS_B * part.astype(F32) + NS_C * square)

    def fill_poly():
        for r in range(4):
            poly[pl.ds(r * step, step), pl.ds(0, width)] = poly_of(r * step, step)

    near = parts // 2
    mine_at = core * near
    last_core = lax.div(f, near)
    f_lanes = pl.ds(pl.multiple_of(lax.rem(f, near) * columns, 128), columns)

    kt = wd.at[pl.ds(0, keys), pl.ds(half + 256, wide_gram)]

    def xo(i):
        return w01.at[1, pl.ds(i * rows, rows)]

    def give():
        return [
            remote(
                sall.at[pl.ds(pl.multiple_of(((1 - core) * near + i) * rows, 16), rows)],
                xo(i), ex_s.at[i], ex_r.at[i], pair,
            )
            for i in range(near)
        ]

    def give_last():
        return remote(x.at[:, f_lanes], xf, fx_s, fx_r, pair)

    @pl.when(p >= 2)
    def _():
        @pl.when(p < WIDE)
        def _():
            x[...] = sall[...]

        @pl.when(p >= WIDE)
        def _():
            copies = give()
            for copy in copies:
                copy.start()
            for i in range(near):
                part = sall[pl.ds(pl.multiple_of((mine_at + i) * rows, 16), rows), :]
                for t in range(2):
                    x[pl.ds(pl.multiple_of(core * tall + t * rows, 16), rows), pl.ds(i * columns, columns)] = part[
                        :, t * columns : (t + 1) * columns
                    ]
            for i, copy in enumerate(copies):
                copy.wait()
                part = xo(i)
                for t in range(2):
                    x[pl.ds(pl.multiple_of((1 - core) * tall + t * rows, 16), rows), pl.ds(i * columns, columns)] = part[
                        :, pl.ds(t * columns, columns)
                    ]

        wide = x[...].astype(F32)
        sq[...] = jnp.broadcast_to(jnp.sum(wide * wide), sq.shape)
        copy = remote(sq, sq_r, qs, qr, pair)
        copy.start()
        copy.wait()
        normal(x, scale_of(sq[...] + sq_r[...])[:1, :1])

        def grams(slot):
            for r in range(4):
                gram_s[pl.ds(r * step, step), pl.ds(0, width)] = rounded(
                    contract(x[pl.ds(r * step, step), :], x[...], 1, 1)
                )
                exchange(slot, r).start()
            for r in range(4):
                part = pl.ds(r * step, step)
                exchange(slot, r).wait()
                g[part, pl.ds(0, width)] = rounded(
                    gram_s[part, pl.ds(0, width)].astype(F32) + gram_r(slot)[part, pl.ds(0, width)].astype(F32)
                )

        def iterate(slot):
            grams(slot)
            fill_poly()
            for tile in range(half // 256):
                part = pl.ds(tile * 256, 256)
                x[:, part] = rounded(
                    NS_A * x[:, part].astype(F32) + jnp.dot(poly[:, pl.ds(0, width)], x[:, part], preferred_element_type=F32)
                )

        def iterate_twice(it, carry):
            iterate(0)
            iterate(1)
            return carry

        lax.fori_loop(0, (NS_ITERS - 1) // 2, iterate_twice, 0)

        @pl.when((p >= WIDE) & (core == last_core))
        def _():
            give_last().start()
            xf[...] = x[:, f_lanes]

        grams(0)

        @pl.when(p < WIDE)
        def _():
            part = poly_of(pl.multiple_of(f * rows, 16), rows)
            pa[...] = rounded(NS_A * x[my_rows, :].astype(F32) + jnp.dot(part, x[...], preferred_element_type=F32))

        @pl.when(p >= WIDE)
        def _():
            pl.when(core == last_core)(lambda: give_last().wait_send())
            pl.when(core != last_core)(lambda: give_last().wait_recv())
            for t in range(2):
                top = pl.multiple_of(core * tall + t * rows, 16)
                part = poly_of(top, rows)
                pa[:, t * columns : (t + 1) * columns] = rounded(
                    NS_A * xf[pl.ds(top, rows), :].astype(F32) + jnp.dot(part, xf[...], preferred_element_type=F32)
                )

    @pl.when(p < 2)
    def _():
        x[...] = sall[...]
        kt[:, pl.ds(0, width)] = x[:, pl.ds(width, keys)].T
        turned = kt[:, pl.ds(0, width)].astype(F32)
        kt[:, pl.ds(0, width)] = rounded(turned * scale_of(jnp.sum(turned * turned)))
        wide = x[:, pl.ds(0, width)].astype(F32)
        x[:, pl.ds(0, width)] = rounded(wide * scale_of(jnp.sum(wide * wide)))

        def narrow_step(it, carry):
            now = kt[:, pl.ds(0, width)]
            gram = rounded(contract(now, now, 1, 1))
            turned = rounded(NS_B * gram.astype(F32) + NS_C * jnp.dot(gram, gram, preferred_element_type=F32))
            kt[:, pl.ds(0, width)] = rounded(
                NS_A * now.astype(F32) + jnp.dot(turned, now, preferred_element_type=F32)
            )
            return carry

        lax.fori_loop(0, NS_ITERS, narrow_step, 0)

        def gram_of():
            for r in range(4):
                part = pl.ds(r * step, step)
                g[part, pl.ds(0, width)] = rounded(contract(x[part, pl.ds(0, width)], x[:, pl.ds(0, width)], 1, 1))

        def square_step(it, carry):
            gram_of()
            fill_poly()
            x[:, pl.ds(0, width)] = rounded(
                NS_A * x[:, pl.ds(0, width)].astype(F32) + jnp.dot(poly[:, pl.ds(0, width)], x[:, pl.ds(0, width)], preferred_element_type=F32)
            )
            return carry

        lax.fori_loop(0, NS_ITERS - 1, square_step, 0)
        gram_of()
        part = poly_of(pl.multiple_of(f * rows, 16), rows)
        square = rounded(
            NS_A * x[my_rows, pl.ds(0, width)].astype(F32) + jnp.dot(part, x[:, pl.ds(0, width)], preferred_element_type=F32)
        )
        x[:, pl.ds(width, keys)] = kt[:, pl.ds(0, width)].T
        pa[:, :width] = square
        pa[:, width:] = x[my_rows, pl.ds(width, keys)]

    out_on, out_finish = spread_even(at, pa, o_out, og_l, og_s, og_r)
    total = gain_s[3]
    for j in range(1, parts):
        line_gain[j - 1].wait()
        total = total + gain_r[3 + j]
    gain_out[...] = total
    finish()
    out_on()
    for copy in sent:
        copy.wait_send()
    out_finish()


def step_pass(x, up, gains, tables, bias, shards, moments):
    parts = lax.axis_size("fsdp")
    width, tokens = x.shape
    half = shards[4].shape[1] // 2
    rows = width // parts
    keys = half - width
    near = parts // 2
    dma = pltpu.SemaphoreType.DMA
    vm = pltpu.VMEM
    group = HEADS // KV_HEADS
    two = 2 * keys
    n_gain = 3 + parts
    return pl.pallas_call(
        step_kernel,
        out_shape=(
            jax.ShapeDtypeStruct((width, tokens), BF16),
            jax.ShapeDtypeStruct((width, tokens), F32),
            jax.ShapeDtypeStruct((CLASSES, rows, half), BF16),
            jax.ShapeDtypeStruct((CLASSES, rows, half), BF16),
            jax.ShapeDtypeStruct((8, width), F32),
        ),
        in_specs=[VMEM] * 11 + [ANY] * 10,
        out_specs=(VMEM, VMEM, ANY, ANY, VMEM),
        scratch_shapes=[
            vm((2, width, half), BF16),
            vm((width, 2 * half), BF16),
            vm((width, 2 * half), BF16),
            vm((width, 2 * half), BF16),
            vm((KV_HEADS, CLASSES * tokens, group * tokens), F32),
            vm((CLASSES, tokens, two), BF16),
            vm((tokens, half), BF16),
            vm((CLASSES, tokens, two), F32),
            vm((2, tokens, 2 * two), BF16),
            vm((2, tokens, 2 * two), BF16),
            vm((1, tokens, 2 * two), BF16),
            vm((1, tokens, two), BF16),
            vm((tokens, width), BF16),
            vm((tokens, 2 * half), F32),
            vm((2 * tokens, half), F32),
            vm((4, width, tokens), BF16),
            vm((CLASSES, tokens, half), BF16),
            vm((tokens, -(-keys // 128) * 128), BF16),
            vm((width, CLASSES * tokens), BF16),
            vm((width, CLASSES * tokens), BF16),
            vm((CLASSES * tokens, half), BF16),
            vm((CLASSES * tokens, -(-keys // 128) * 128), BF16),
            vm((parts - 1, rows, half), BF16),
            vm((rows, half), F32),
            vm((rows, width), F32),
            vm((keys, rows), F32),
            vm((4, 8, width), F32),
            vm((n_gain, 8, width), F32),
            vm((8, 128), F32),
            vm((8, 128), F32),
            dma((3,)), dma((4, parts)), dma((4, parts)), dma((4, 2, parts)), dma((4, 4, parts)),
            dma((4, CLASSES, parts)), dma((7,)), dma((CLASSES,)), dma((3,)), dma((3,)),
            dma((4,)), dma((CLASSES,)), dma((CLASSES,)), dma((CLASSES,)), dma((CLASSES,)),
            dma((CLASSES,)), dma((CLASSES,)), dma, dma((CLASSES,)), dma, dma((CLASSES,)),
            dma((2,)), dma((2,)), dma((parts,)), dma((parts,)),
            dma((2,)), dma((n_gain,)), dma((n_gain,)),
            dma, dma((7,)), dma((CLASSES,)),
            dma((parts,)), dma((parts,)), dma((parts,)), dma((parts,)),
            dma((4,)), dma((2, 4)), dma, dma,
            dma((near,)), dma((near,)), dma, dma,
            dma, dma((7,)), dma((CLASSES,)), pltpu.SemaphoreType.REGULAR((2,)),
        ],
        compiler_params=pltpu.CompilerParams(
            collective_id=3, has_side_effects=True, vmem_limit_bytes=63 << 20
        ),
        name="step_pass",
    )(x, up, gains, *tables, bias, *shards, *moments)


def settle_wide(factors, *refs):
    gs, os = refs[0], refs[1]
    ms, ws, outs = refs[2:6], refs[6:10], refs[10:]
    width = ms[0].shape[1]
    half = gs.shape[2]

    def one(index, g, o, lanes):
        grad, moment, weight = (outs[3 * index + i] for i in range(3))
        value = g.astype(F32)
        grad[:, lanes] = value
        moment[:, lanes] = MOMENTUM * ms[index][:, lanes] + value
        weight[:, lanes] = ws[index][:, lanes].astype(F32) + factors[index] * o.astype(F32)

    for index in range(2):
        one(index, gs[index, :, :width], os[index, :, :width], slice(0, width))
    for index in range(2):
        for side in range(2):
            cls = 2 + 2 * index + side
            one(2 + index, gs[cls], os[cls], slice(side * half, (side + 1) * half))


def settle_turned(factors, g_tall, o_tall, g_pair, o_pair, *refs):
    ms, ws, outs = refs[0:3], refs[3:6], refs[6:]
    keys = ms[1].shape[0]

    def one(index, g, o):
        grad, moment, weight = (outs[3 * index + i] for i in range(3))
        grad[...] = g
        moment[...] = MOMENTUM * ms[index][...] + g
        weight[...] = ws[index][...].astype(F32) + factors[index] * o

    one(0, g_tall[0].astype(F32), o_tall[0].astype(F32))

    @pl.when(pl.program_id(0) == 0)
    def _():
        for index in range(2):
            start = g_pair.shape[2] - keys
            one(1 + index, g_pair[index, :, start:].astype(F32).T, o_pair[index, :, start:].astype(F32).T)


def settle(g, o, moments, shards, factors):
    m_q, m_k, m_o, m_v, m_gate, m_up, m_down = moments
    w_q, w_k, w_o, w_v, w_gate, w_up, w_down = shards
    f_q, f_k, f_v, f_o, f_gate, f_up, f_down = factors
    _, rows, half = g.shape
    width, columns = m_down.shape
    block = 48 if rows % 48 == 0 else rows
    piece = pl.BlockSpec((WIDE, block, half), lambda i: (0, i, 0))

    def row_block(array):
        return pl.BlockSpec((block, array.shape[1]), lambda i: (i, 0))

    def result(arrays):
        return tuple(jax.ShapeDtypeStruct(array.shape, F32) for array in arrays for _ in range(3))

    wide = (m_q, m_o, m_gate, m_up)
    first = pl.pallas_call(
        functools.partial(settle_wide, (f_q, f_o, f_gate, f_up)),
        grid=(rows // block,),
        out_shape=result(wide),
        in_specs=[piece, piece] + [row_block(array) for array in wide] * 2,
        out_specs=tuple(row_block(array) for array in wide for _ in range(3)),
        compiler_params=pltpu.CompilerParams(vmem_limit_bytes=48 << 20),
        name="settle_wide",
    )(g, o, *wide, w_q, w_o, w_gate, w_up)

    turned = (m_down, m_k, m_v)
    halves = half // columns
    tile = pl.BlockSpec((1, rows, columns), lambda i: (WIDE + i // halves, 0, i % halves))
    both = pl.BlockSpec((2, rows, half), lambda i: (0, 0, 0))
    specs = [pl.BlockSpec((rows, columns), lambda i: (i, 0))] + [
        pl.BlockSpec(array.shape, lambda i: (0, 0)) for array in turned[1:]
    ]
    second = pl.pallas_call(
        functools.partial(settle_turned, (f_down, f_k, f_v)),
        grid=(width // rows,),
        out_shape=result(turned),
        in_specs=[tile, tile, both, both] + specs * 2,
        out_specs=tuple(spec for spec in specs for _ in range(3)),
        compiler_params=pltpu.CompilerParams(vmem_limit_bytes=48 << 20),
        name="settle_turned",
    )(g, o, g, o, *turned, w_down, w_k, w_v)
    q, out, gate, up = (first[3 * i : 3 * i + 3] for i in range(4))
    down, k, v = (tuple(item.T for item in second[3 * i : 3 * i + 3]) for i in range(3))
    return list(zip(q, k, v, out, gate, up, down))


def rotary_tables(positions, width):
    half = width // 2
    frequency = THETA ** (-(jnp.arange(half, dtype=jnp.float32) * 2.0 / width))
    angle = positions.astype(jnp.float32)[:, None] * frequency[None, :]
    return (jnp.cos(angle)[:, None, :], jnp.sin(angle)[:, None, :])


def rotate(value, cosine, sine):
    half = value.shape[-1] // 2
    first = value[..., :half]
    second = value[..., half:]
    return jnp.concatenate(
        [first * cosine - second * sine, second * cosine + first * sine], axis=-1
    )


def unrotate(incoming, cosine, sine):
    half = incoming.shape[-1] // 2
    upper = incoming[..., :half]
    lower = incoming[..., half:]
    return jnp.concatenate([upper * cosine + lower * sine, lower * cosine - upper * sine], axis=-1)


def norm_forward(residual, gain):
    inverse = lax.rsqrt(jnp.mean(residual * residual, axis=-1, keepdims=True) + EPS)
    return ((residual * inverse * gain).astype(jnp.bfloat16), inverse)


def norm_backward(residual, inverse, gain, incoming):
    scaled = incoming * gain
    through = inverse * scaled - residual * inverse**3 * jnp.mean(
        scaled * residual, axis=-1, keepdims=True
    )
    return (through, jnp.sum(incoming * residual * inverse, axis=0))


def padded(array, axis, parts, count, full):
    if count == full:
        return array
    shape = array.shape
    split = array.reshape(shape[:axis] + (parts, count) + shape[axis + 1 :])
    pads = [(0, 0)] * split.ndim
    pads[axis + 1] = (0, full - count)
    return jnp.pad(split, pads).reshape(shape[:axis] + (parts * full,) + shape[axis + 1 :])


def trimmed(array, axis, parts, count, full):
    if count == full:
        return array
    shape = array.shape
    split = array.reshape(shape[:axis] + (parts, full) + shape[axis + 1 :])
    kept = lax.slice_in_dim(split, 0, count, axis=axis + 1)
    return kept.reshape(shape[:axis] + (parts * count,) + shape[axis + 1 :])


def plain_layer(
    layer_input, output_grad, wide, tall, norm_gains, block_order, sizes
):
    parts, width, half, kv, short, full, high = sizes
    hidden_size = 2 * half
    rows = layer_input.shape[1]
    block = rows // 2
    group = HEADS // KV_HEADS
    scale = 1.0 / math.sqrt(HEAD)
    ctx_place = lax.axis_index("ctx")
    offsets = jnp.arange(block, dtype=jnp.int32)
    own_blocks = lax.dynamic_slice_in_dim(block_order, 2 * ctx_place, 2)
    query_pos = (own_blocks[:, None] * block + offsets[None, :]).reshape(rows)
    key_pos = (block_order[:, None] * block + offsets[None, :]).reshape(-1)

    all_wide, all_tall = gather_weights(wide, tall)
    w_qk, w_ov, w_gate_0, w_gate_1, w_up_0, w_up_1 = [all_wide[i].reshape(width, half) for i in range(WIDE)]
    w_down = [all_tall[i].reshape(half, width) for i in range(2)]

    residual = layer_input[0].astype(jnp.float32)
    normed_first, inverse_first = norm_forward(residual, norm_gains[0])
    qk_pre = jnp.dot(normed_first, w_qk, preferred_element_type=jnp.float32)
    query_pre = qk_pre[:, :width].reshape(rows, HEADS, HEAD)
    key_pre = qk_pre[:, width:].reshape(rows, KV_HEADS, HEAD)
    value_low = (
        jnp.dot(normed_first, w_ov, preferred_element_type=jnp.float32)[:, width:]
        .astype(jnp.bfloat16)
        .reshape(rows, KV_HEADS, HEAD)
    )
    cosine, sine = rotary_tables(query_pos, HEAD)
    query_rot = rotate(query_pre, cosine, sine).astype(jnp.bfloat16)
    key_rot = rotate(key_pre, cosine, sine).astype(jnp.bfloat16)
    keys_all, values_all = (
        lax.all_gather(key_rot, "ctx", axis=0, tiled=True),
        lax.all_gather(value_low, "ctx", axis=0, tiled=True),
    )
    keys_head = keys_all.transpose(1, 0, 2)
    values_head = values_all.transpose(1, 0, 2)
    queries_head = (
        query_rot.reshape(rows, KV_HEADS, group, HEAD)
        .transpose(1, 2, 0, 3)
        .reshape(KV_HEADS, group * rows, HEAD)
    )
    row_pos = jnp.tile(query_pos, group)
    allowed = key_pos[None, :] <= row_pos[:, None]

    def head_forward(item):
        query, key, value = item
        scores = jnp.where(allowed, contract(query, key, 1, 1) * scale, MASKED)
        top = jnp.max(scores, axis=-1, keepdims=True)
        expo = jnp.exp(scores - top)
        total = jnp.sum(expo, axis=-1, keepdims=True)
        probs_low = (expo / total).astype(jnp.bfloat16)
        return (
            jnp.dot(probs_low, value, preferred_element_type=jnp.float32),
            (top + jnp.log(total))[:, 0],
        )

    mixed, log_total = lax.map(head_forward, (queries_head, keys_head, values_head))
    attended = (
        mixed.reshape(KV_HEADS, group, rows, HEAD)
        .transpose(2, 0, 1, 3)
        .reshape(rows, HEADS * HEAD)
        .astype(jnp.bfloat16)
    )
    w_out = w_ov[:, :width]
    middle = residual + jnp.dot(attended, w_out, preferred_element_type=jnp.float32)
    normed_second, inverse_second = norm_forward(middle, norm_gains[1])

    def sides(left, right):
        return jnp.concatenate([left, right], axis=1)

    gate = sides(
        jnp.dot(normed_second, w_gate_0, preferred_element_type=jnp.float32),
        jnp.dot(normed_second, w_gate_1, preferred_element_type=jnp.float32),
    )
    lifted = sides(
        jnp.dot(normed_second, w_up_0, preferred_element_type=jnp.float32),
        jnp.dot(normed_second, w_up_1, preferred_element_type=jnp.float32),
    )
    sigma = jax.nn.sigmoid(gate)
    hidden = (gate * sigma * lifted).astype(jnp.bfloat16)
    hidden_split = hidden.reshape(rows, parts, 2, high)
    hidden_sides = [hidden_split[:, :, i].reshape(rows, half) for i in range(2)]
    layer_output = (
        middle
        + jnp.dot(hidden_sides[0], w_down[0], preferred_element_type=jnp.float32)
        + jnp.dot(hidden_sides[1], w_down[1], preferred_element_type=jnp.float32)
    ).astype(jnp.bfloat16)
    upstream = output_grad[0]
    grad_hidden = jnp.stack(
        [contract(upstream, w_down[i], 1, 1).reshape(rows, parts, high) for i in range(2)], axis=2
    ).reshape(rows, hidden_size)
    grad_gate = (grad_hidden * lifted * sigma * (1.0 + gate * (1.0 - sigma))).astype(jnp.bfloat16)
    grad_lifted = (grad_hidden * gate * sigma).astype(jnp.bfloat16)
    grad_normed_second = (
        contract(grad_gate[:, :half], w_gate_0, 1, 1)
        + contract(grad_gate[:, half:], w_gate_1, 1, 1)
        + contract(grad_lifted[:, :half], w_up_0, 1, 1)
        + contract(grad_lifted[:, half:], w_up_1, 1, 1)
    )
    through_second, gain_second = norm_backward(
        middle, inverse_second, norm_gains[1], grad_normed_second
    )
    grad_middle = upstream.astype(jnp.float32) + through_second
    grad_branch = grad_middle.astype(jnp.bfloat16)
    grad_attended = contract(grad_branch, w_out, 1, 1).astype(jnp.bfloat16)
    grad_heads = (
        grad_attended.reshape(rows, KV_HEADS, group, HEAD)
        .transpose(1, 2, 0, 3)
        .reshape(KV_HEADS, group * rows, HEAD)
    )

    def head_backward(item):
        query, key, value, grad_out, log_row = item
        scores = jnp.where(allowed, contract(query, key, 1, 1) * scale, MASKED)
        probs = jnp.exp(scores - log_row[:, None])
        grad_value_part = contract(probs.astype(jnp.bfloat16), grad_out, 0, 0)
        grad_probs = contract(grad_out, value, 1, 1)
        grad_scores = (
            probs * (grad_probs - jnp.sum(grad_probs * probs, axis=-1, keepdims=True))
        ).astype(jnp.bfloat16)
        grad_query_part = jnp.dot(grad_scores, key, preferred_element_type=jnp.float32) * scale
        grad_key_part = contract(grad_scores, query, 0, 0) * scale
        return (grad_query_part, grad_key_part, grad_value_part)

    grad_query_rot, grad_key_all, grad_value_all = lax.map(
        head_backward, (queries_head, keys_head, values_head, grad_heads, log_total)
    )
    grad_key_own, grad_value_own = (
        lax.psum_scatter(
            grad_key_all.astype(jnp.bfloat16), "ctx", scatter_dimension=1, tiled=True
        ).astype(jnp.float32),
        lax.psum_scatter(
            grad_value_all.astype(jnp.bfloat16), "ctx", scatter_dimension=1, tiled=True
        ).astype(jnp.float32),
    )
    grad_query = (
        unrotate(
            grad_query_rot.reshape(KV_HEADS, group, rows, HEAD)
            .transpose(2, 0, 1, 3)
            .reshape(rows, HEADS, HEAD),
            cosine,
            sine,
        )
        .reshape(rows, HEADS * HEAD)
        .astype(jnp.bfloat16)
    )
    grad_key = (
        unrotate(grad_key_own.transpose(1, 0, 2), cosine, sine)
        .reshape(rows, KV_HEADS * HEAD)
        .astype(jnp.bfloat16)
    )
    grad_value = (
        grad_value_own.transpose(1, 0, 2).reshape(rows, KV_HEADS * HEAD).astype(jnp.bfloat16)
    )
    grad_qk = sides(grad_query, grad_key)
    zero_query = jnp.zeros((rows, width), jnp.bfloat16)
    grad_v = sides(zero_query, grad_value)
    grad_normed_first = contract(grad_qk, w_qk, 1, 1) + contract(grad_v, w_ov, 1, 1)
    through_first, gain_first = norm_backward(
        residual, inverse_first, norm_gains[0], grad_normed_first
    )
    input_gradient = grad_middle + through_first

    xt = jnp.stack([item.T for item in (normed_first, attended, normed_second, upstream)])
    xt = padded(xt, 1, parts, short, full)
    dy = jnp.stack(
        [
            grad_qk,
            sides(grad_branch, jnp.zeros((rows, kv), jnp.bfloat16)),
            grad_gate[:, :half],
            grad_gate[:, half:],
            grad_lifted[:, :half],
            grad_lifted[:, half:],
            hidden_sides[0],
            hidden_sides[1],
            grad_v,
        ]
    )
    gains = jnp.pad(jnp.stack([gain_first, gain_second]), ((0, 6), (0, 0)))
    return layer_output, input_gradient, xt, dy, gains


def rotation(block_order, rows):
    block = rows // 2
    ctx_place = lax.axis_index("ctx")
    offsets = jnp.arange(block, dtype=jnp.int32)
    own_blocks = lax.dynamic_slice_in_dim(block_order, 2 * ctx_place, 2)
    query_pos = (own_blocks[:, None] * block + offsets[None, :]).reshape(rows)
    key_pos = (block_order[:, None] * block + offsets[None, :]).reshape(-1)
    bias = jnp.where(key_pos[:, None] <= query_pos[None, :], 0.0, MASKED).astype(jnp.bfloat16)
    lane = jnp.arange(128, dtype=jnp.int32)
    index = (lane % (HEAD // 2)).astype(jnp.float32)
    frequency = THETA ** (-(index * 2.0 / HEAD))
    angle = query_pos.astype(jnp.float32)[:, None] * frequency[None, :]
    cosine, sine = jnp.cos(angle), jnp.sin(angle)
    early = (lane % HEAD < HEAD // 2)[None, :]
    return (cosine, jnp.where(early, 0.0, sine), jnp.where(early, -sine, 0.0)), bias


def plain_step(layer_input, output_grad, norm_gains, block_order, weights, olds, factors, sizes):
    parts, width, half, kv, short, full, high = sizes
    query_weight, key_weight, value_weight, output_weight, gate_weight, up_weight, down_weight = weights
    (
        query_momentum,
        key_momentum,
        value_momentum,
        output_momentum,
        gate_momentum,
        up_momentum,
        down_momentum,
    ) = olds

    def sides(left, right):
        return jnp.concatenate([left, right], axis=1)

    wide = jnp.stack(
        [
            jnp.concatenate([query_weight, key_weight], axis=1),
            jnp.concatenate([output_weight, value_weight], axis=1),
            gate_weight[:, :half],
            gate_weight[:, half:],
            up_weight[:, :half],
            up_weight[:, half:],
        ]
    )
    tall = down_weight.reshape(2, high, width)
    layer_output, input_gradient, xt, dy, gains = plain_layer(
        layer_input, output_grad, wide, tall, norm_gains, block_order, sizes
    )

    def pad_rows(array):
        return padded(array, 0, 1, short, full)

    def pad_columns(array):
        return padded(array, 1, parts, short, full)

    moments = (
        pad_rows(sides(query_momentum, key_momentum)),
        pad_rows(sides(output_momentum, value_momentum)),
        pad_rows(gate_momentum),
        pad_rows(up_momentum),
        pad_columns(down_momentum),
    )
    g_wide, g_tall, s_wide, s_tall, gain_sum = reduce_gradients(xt, dy, gains, moments, full, high)
    o_wide, o_tall = orthogonalize(s_wide, s_tall, full, high, width)

    def unpack(wide_pieces, tall_pieces):
        pieces = wide_pieces[:, :short]
        tall = trimmed(tall_pieces, 2, parts, short, full).reshape(2 * high, width)
        return (
            pieces[0, :, :width],
            pieces[0, :, width:],
            pieces[1, :, width:],
            pieces[1, :, :width],
            sides(pieces[2], pieces[3]),
            sides(pieces[4], pieces[5]),
            tall,
        )

    gradients = [item.astype(jnp.float32) for item in unpack(g_wide, g_tall)]
    orthos = unpack(o_wide, o_tall)
    moments = [MOMENTUM * old + new for old, new in zip(olds, gradients)]
    new_weights = [
        weight.astype(jnp.float32) + factor * ortho.astype(jnp.float32)
        for weight, factor, ortho in zip(weights, factors, orthos)
    ]
    return layer_output, input_gradient, gradients, moments, new_weights, gain_sum


def on_device(
    layer_input,
    output_grad,
    query_weight,
    key_weight,
    value_weight,
    output_weight,
    gate_weight,
    up_weight,
    down_weight,
    norm_gains,
    query_momentum,
    key_momentum,
    value_momentum,
    output_momentum,
    gate_momentum,
    up_momentum,
    down_momentum,
    gain_momentum,
    block_order,
):
    parts = lax.axis_size("fsdp")
    width = layer_input.shape[2]
    half = gate_weight.shape[1] // 2
    kv = key_weight.shape[1]
    short = width // parts
    full = -(-short // 16) * 16
    high = half // parts
    sizes = (parts, width, half, kv, short, full, high)

    weights = (query_weight, key_weight, value_weight, output_weight, gate_weight, up_weight, down_weight)
    olds = (
        query_momentum,
        key_momentum,
        value_momentum,
        output_momentum,
        gate_momentum,
        up_momentum,
        down_momentum,
    )
    factors = []
    for index, weight in enumerate(weights):
        step_rate = OUT_RATE if index == 3 else RATE
        factors.append(-step_rate * max(1.0, weight.shape[1] / (weight.shape[0] * parts)) ** 0.5)

    fused = (
        lax.axis_size("ctx") == CLASSES
        and short == full
        and parts % 2 == 0
        and half % (2 * half // parts) == 0
        and (2 * half // parts) % 128 == 0
        and layer_input.shape[1] == 128
        and short <= 256
    )
    if fused:
        tables, bias = rotation(block_order, layer_input.shape[1])

        def turned(items):
            q, k, v, o, gate, up, down = items
            return (q, k.T, o, v.T, gate, up, down.T)

        shards, moments = turned(weights), turned(olds)
        out_turned, grad_turned, g, o, gain_sum = step_pass(
            layer_input[0].T, output_grad[0].T, norm_gains, tables, bias, shards, moments
        )
        gradients, moments, new_weights = settle(g, o, moments, shards, factors)
        layer_output, input_gradient = out_turned.T, grad_turned.T
    else:
        layer_output, input_gradient, gradients, moments, new_weights, gain_sum = plain_step(
            layer_input, output_grad, norm_gains, block_order, weights, olds, factors, sizes
        )
    gain_width = norm_gains.shape[1] // parts
    place = lax.axis_index("fsdp") * gain_width
    gain_gradient = lax.dynamic_slice_in_dim(gain_sum[:2], place, gain_width, 1)
    gain_shard = lax.dynamic_slice_in_dim(norm_gains, place, gain_width, 1)
    gain_moment = MOMENTUM * gain_momentum + gain_gradient
    new_gains = gain_shard - GAIN_RATE * gain_moment
    return (
        layer_output[None],
        input_gradient[None],
        *gradients,
        gain_gradient,
        *moments,
        gain_moment,
        *new_weights,
        new_gains,
    )


def solution(mesh):
    tokens = P("fsdp", "ctx", None)
    shard = P("fsdp", None)
    gains = P(None, "fsdp")
    return jax.shard_map(
        on_device,
        mesh=mesh,
        in_specs=(tokens, tokens) + (shard,) * 7 + (P(),) + (shard,) * 7 + (gains, P()),
        out_specs=(tokens, tokens) + ((shard,) * 7 + (gains,)) * 3,
        check_vma=False,
    )
```

profile of v0, /device:TPU:3, one launch (start us, length us, event | category | flops | bytes accessed | tf_op | source)
XLA Modules:
  0.0 390.2 jit_solution(1044310089889065297)
XLA Ops:
  0.7 0.7 dynamic-slice_multiply_fusion
  1.4 0.1 iota_add_fusion.1
  1.5 0.1 add.79
  1.6 0.7 broadcast_multiply_fusion
  2.2 0.1 iota_add_fusion
  2.3 0.1 add.85
  2.4 1.0 fusion.2
  3.4 0.9 select_convert_fusion.bias_ref
  4.3 359.2 %step_pass.1 = (bf16[960,128]{1,0:T(8,128)(2,1)}, f32[960,128]{1,0:T(8,128)}, bf16[8,240,1280]{2,1,0:T(8,128)(2,1)}, bf16[8,240,1280]{2,1,0:T(8,128)(2,1)}, f32[8,960]{1,0:T(8,128)}) custom-call(bf16[960,128]{1,0:T(8,128)(2,1)} %bitcast.41, bf16[960,128]{1,0:T(8,128)(2,1)} %bitcast.42, f32[2,960]{1,0:T(2,128)} %gains_ref.1, ...), custom_call_target="tpu_custom_call" | custom-call | tf_op jit(solution)/shard_map/step_pass/pallas_call | solution.py:1578
  363.5 0.8 slice.3
  364.2 1.4 multiply_subtract_fusion
  365.6 0.0 copy-done.8
  365.6 0.0 copy-done.9
  365.6 0.0 copy-done.10
  365.6 0.0 copy-done.11
  365.6 0.0 copy-start
  365.6 1.7 copy-done
  367.3 1.3 copy-done.3
  368.6 0.0 copy-start.6
  368.6 0.0 copy-start.7
  368.6 7.3 %settle_turned.1 = (f32[960,640]{1,0:T(8,128)}, f32[960,640]{1,0:T(8,128)}, f32[960,640]{1,0:T(8,128)}, f32[320,240]{1,0:T(8,128)}, f32[320,240]{1,0:T(8,128)}, ...) custom-call(bf16[8,240,1280]{2,1,0:T(8,128)(2,1)} %get-tuple-element.54.refs_0_.g_tall.g_pair,, ...), custom_call_target="tpu_custom_call" | custom-call | tf_op jit(solution)/shard_map/settle_turned/pallas_call | solution.py:1712
  376.0 12.2 %settle_wide.1 = (f32[240,960]{1,0:T(8,128)}, f32[240,960]{1,0:T(8,128)}, f32[240,960]{1,0:T(8,128)}, f32[240,960]{1,0:T(8,128)}, f32[240,960]{1,0:T(8,128)}, /*...) custom-call(bf16[8,240,1280]{2,1,0:T(8,128)(2,1)} %get-tuple-element, ...), custom_call_target="tpu_custom_call" | custom-call | tf_op jit(solution)/shard_map/settle_wide/pallas_call | solution.py:1695
  388.2 0.7 copy.47
  388.9 0.8 copy.48
  (22 shorter events, 0.1 us)
Async XLA Ops:
  4.3 361.3 %copy-start.8 = (f32[240,320]{0,1:T(8,128)S(1)}, f32[240,320]{0,1:T(8,128)}, u32[]{:S(2)}) copy-start(f32[240,320]{0,1:T(8,128)} %param.30) | copy-start | bytes 921604
  4.3 361.3 %copy-start.9 = (f32[240,320]{0,1:T(8,128)S(1)}, f32[240,320]{0,1:T(8,128)}, u32[]{:S(2)}) copy-start(f32[240,320]{0,1:T(8,128)} %param.31) | copy-start | bytes 921604
  4.3 361.3 %copy-start.10 = (bf16[240,320]{0,1:T(8,128)(2,1)S(1)}, bf16[240,320]{0,1:T(8,128)(2,1)}, u32[]{:S(2)}) copy-start(bf16[240,320]{0,1:T(8,128)(2,1)} %param.22) | copy-start | bytes 460804
  4.3 361.3 %copy-start.11 = (bf16[240,320]{0,1:T(8,128)(2,1)S(1)}, bf16[240,320]{0,1:T(8,128)(2,1)}, u32[]{:S(2)}) copy-start(bf16[240,320]{0,1:T(8,128)(2,1)} %param.23) | copy-start | bytes 460804
  365.6 1.7 copy-start
  367.3 1.3 copy-start.3
  368.6 7.4 %copy-start.1 = (bf16[240,2560]{1,0:T(8,128)(2,1)S(1)}, bf16[240,2560]{1,0:T(8,128)(2,1)}, u32[]{:S(2)}) copy-start(bf16[240,2560]{1,0:T(8,128)(2,1)} %refs_8_.1) | copy-start | bytes 3686404
  368.6 7.4 %copy-start.2 = (bf16[240,2560]{1,0:T(8,128)(2,1)S(1)}, bf16[240,2560]{1,0:T(8,128)(2,1)}, u32[]{:S(2)}) copy-start(bf16[240,2560]{1,0:T(8,128)(2,1)} %refs_9_.1) | copy-start | bytes 3686404
  368.6 7.4 %copy-start.4 = (f32[240,960]{1,0:T(8,128)S(1)}, f32[240,960]{1,0:T(8,128)}, u32[]{:S(2)}) copy-start(f32[240,960]{1,0:T(8,128)} %refs_2_.1) | copy-start | bytes 2764804
  368.6 7.4 %copy-start.5 = (f32[240,960]{1,0:T(8,128)S(1)}, f32[240,960]{1,0:T(8,128)}, u32[]{:S(2)}) copy-start(f32[240,960]{1,0:T(8,128)} %refs_3_.1) | copy-start | bytes 2764804
  368.6 7.4 %copy-start.6 = (bf16[240,960]{1,0:T(8,128)(2,1)S(1)}, bf16[240,960]{1,0:T(8,128)(2,1)}, u32[]{:S(2)}) copy-start(bf16[240,960]{1,0:T(8,128)(2,1)} %refs_6_.1) | copy-start | bytes 1382404
  368.6 7.4 %copy-start.7 = (bf16[240,960]{1,0:T(8,128)(2,1)S(1)}, bf16[240,960]{1,0:T(8,128)(2,1)}, u32[]{:S(2)}) copy-start(bf16[240,960]{1,0:T(8,128)(2,1)} %refs_7_.1) | copy-start | bytes 1382404
  376.0 12.2 %copy-start.13 = (bf16[960,128]{1,0:T(8,128)(2,1)S(1)}, bf16[960,128]{1,0:T(8,128)(2,1)}, u32[]{:S(2)}) copy-start(bf16[960,128]{1,0:T(8,128)(2,1)} %get-tuple-element.52) | copy-start | bytes 737284
  376.0 12.9 %copy-start.12 = (f32[960,128]{1,0:T(8,128)S(1)}, f32[960,128]{1,0:T(8,128)}, u32[]{:S(2)}) copy-start(f32[960,128]{1,0:T(8,128)} %get-tuple-element.53) | copy-start | bytes 1474564
where the time goes:
time: 398 us; the launch traced here: 390 us
  Pallas kernels  379 us (95%)
  local copies, waits for them, and re-layouts  5.42 us (1%)
  other arithmetic  4.81 us (1%)
    pallas_call x1, Pallas kernels, step_pass(): pl.pallas_call(step_kernel, out_shape=(jax.ShapeDtypeStruct((width, token...  359 us
    pallas_call x1, Pallas kernels, settle(): pl.pallas_call(functools.partial(settle_wide, (f_q, f_o, f_gate, f_up)),...  12.2 us

commit v1 on v0

--- a/solution.py
+++ b/solution.py
@@ -1066,7 +1066,7 @@
         lanes = slice(side * half, (side + 1) * half)
         dy_in[2 + side] = grad_gate[:, lanes]
         dy_in[4 + side] = grad_lifted[:, lanes]
-    for bits in (1, at.b1, at.b1 ^ 1, at.b2, at.b2 ^ 1):
+    for bits in range(1, CLASSES):
         give_y(bits, 2, WIDE)
 
     out_ref[...] = (middle + contract(hidden, wd[...], 1, 1)).T.astype(BF16)
@@ -1089,7 +1089,7 @@
     dy_in[1, :, width:] = jnp.zeros((tokens, keys), BF16)
     att[...] = contract(grad_branch, w01[1, :, :width], 1, 1).astype(BF16)
 
-    for bits in (1, at.b1, at.b1 ^ 1, at.b2, at.b2 ^ 1):
+    for bits in range(1, CLASSES):
         give_y(bits, 1, 2)
 
     own = lifted.at[pl.ds(0, rows)]
@@ -1100,14 +1100,25 @@
     def order(i):
         return lax.rem(f + 1 + i, parts)
 
+    cut = width // 128 * 128
+    part_lanes = (pl.ds(0, cut), pl.ds(cut, half - cut))
+    parts_early = (lambda: p >= 1, lambda: p >= 2)
+    parts_late = (lambda: p < 1, lambda: p < 2)
+
     def room(r):
         return wd.at[pl.ds(pl.multiple_of(r * rows, 16), rows), pl.ds(half, half)]
 
-    def line(r, source):
-        return remote(room(r), za_r.at[(r ^ source) - 1], ozs.at[r], ozr.at[source], (at.c, r))
-
-    def arrival(j):
-        return remote(room(f), za_r.at[j - 1], ozs.at[f], ozr.at[f ^ j], at.along(j))
+    def line(r, source, part):
+        lanes = part_lanes[part]
+        return remote(
+            room(r).at[:, lanes], za_r.at[(r ^ source) - 1, :, lanes], ozs.at[part, r], ozr.at[part, source], (at.c, r)
+        )
+
+    def arrival(j, part):
+        lanes = part_lanes[part]
+        return remote(
+            room(f).at[:, lanes], za_r.at[j - 1, :, lanes], ozs.at[part, f], ozr.at[part, f ^ j], at.along(j)
+        )
 
     middle_token = CLASSES // 2 * tokens
 
@@ -1127,9 +1138,7 @@
 
         @pl.when(p == 1)
         def _():
-            value = jnp.dot(xf_all[at_rows, :], yv_all[...], preferred_element_type=F32)
             put(slice(0, width), jnp.dot(xa_all[at_rows, :], yf_all[:, pl.ds(0, width)], preferred_element_type=F32))
-            put(slice(width, half), value[:, :keys])
 
         @pl.when((p != 1) & (p < WIDE))
         def _():
@@ -1165,34 +1174,51 @@
                         ),
                     )
 
-    def gradients():
+    def keep_chunk(r):
+        def put(lanes, value):
+            own[:, lanes] = value
+            room(r)[:, lanes] = value.astype(BF16)
+
+        return put
+
+    def gradients(conditions):
         for bits in range(1, CLASSES):
             arrived_y(p ^ bits)
 
         @pl.when(p >= WIDE)
         def _():
-            pl.semaphore_wait(free.at[0], 1)
             for copy in sides_of():
                 copy.start()
             for copy in sides_of():
                 copy.wait()
 
-        @pl.when(p < WIDE)
-        def _():
-            pl.semaphore_wait(free.at[0], 1)
-
         def step_of(i, carry):
             r = order(i)
-
-            def put(lanes, value):
-                own[:, lanes] = value
-                room(r)[:, lanes] = value.astype(BF16)
-
-            produce(r, put)
+            produce(r, keep_chunk(r))
+            for part in range(2):
+                pl.when((i < parts - 1) & conditions[part]())(lambda part=part: line(r, f, part).start())
+            return carry
+
+        lax.fori_loop(0, parts, step_of, 0)
+
+    def value_gradient():
+        for q in range(CLASSES):
+            if q != 1:
+                remote(dv_in, yv_all.at[tokens_of(q)], vs, vr.at[q], pair).wait_recv()
+
+        def step_of(i, carry):
+            r = order(i)
+            at_rows = pl.ds(pl.multiple_of(r * rows, 16), rows)
+            value = jnp.dot(xf_all[at_rows, :], yv_all[...], preferred_element_type=F32)
 
             @pl.when(i < parts - 1)
             def _():
-                line(r, f).start()
+                room(r)[:, pl.ds(width, keys)] = value[:, :keys].astype(BF16)
+                line(r, f, 1).start()
+
+            @pl.when(i == parts - 1)
+            def _():
+                own[:, pl.ds(width, keys)] = value[:, :keys]
 
             return carry
 
@@ -1238,13 +1264,36 @@
         for i, bits in enumerate(rest):
             dkv[p ^ bits] = dkv[p ^ bits] + rbuf[i // 2, :, pl.ds(i % 2 * 2 * keys, 2 * keys)].astype(F32)
 
-    def diagonal():
-        for bits in (at.b1 ^ at.b2, at.b1 ^ at.b2 ^ 1):
-            give_y(bits, 1, WIDE)
+    own_x.wait()
+    for bits in (2, 4, 6):
+        arrived_x(p ^ bits)
+    for bits in (0, 2, 4, 6):
+        x_pair(bits).start()
+
+    def early():
+        for bits in (0, 2, 4, 6):
+            remote(
+                xf_all.at[:, tokens_of(p ^ bits ^ 1)], xf_all.at[:, tokens_of(p ^ bits ^ 1)],
+                ps.at[bits], pr.at[p ^ bits ^ 1], pair,
+            ).wait_recv()
+        pl.semaphore_wait(free.at[0], 1)
+
+        @pl.when(p == 1)
+        def _():
+            own_a().wait()
+            for q in range(CLASSES):
+                if q != 1:
+                    remote(xt_in.at[1], xa_all.at[:, tokens_of(q)], as_, ar.at[q], pair).wait_recv()
+
+        @pl.when(p >= 1)
+        def _():
+            own_y().start()
+            own_y().wait()
+            gradients(parts_early)
 
     halve(1, (0, 2, 4, 6), c_send, c4r, 0)
-    halve(at.b1, (0, at.b2), c4r.at[pl.ds(0, 1)], c2r, 1)
-    halve(at.b2, (0,), c4r.at[pl.ds(1, 1), :, pl.ds(0, 2 * keys)], c1r, 2, diagonal)
+    halve(at.b1, (0, at.b2), c4r.at[pl.ds(0, 1)], c2r, 1, early)
+    halve(at.b2, (0,), c4r.at[pl.ds(1, 1), :, pl.ds(0, 2 * keys)], c1r, 2)
 
     gate[:, width:half] = dkv[p, :, :keys]
     for tile, value in enumerate(turn(gate[:, :half], -1)):
@@ -1255,14 +1304,6 @@
         give_y(bits, 0, 1)
     pl.when(p != 1)(lambda: v_move().start())
     pl.when(p == 1)(lambda: own_v().start())
-    own_y().start()
-
-    own_x.wait()
-    for bits in (2, 4, 6):
-        arrived_x(p ^ bits)
-    for bits in (0, 2, 4, 6):
-        x_pair(bits).start()
-
     grad_normed = contract(dy_in[0], w01[0], 1, 1)
     grad_normed = grad_normed + contract(dv_in[:, :keys], w01[1, :, width:], 1, 1)
     through, gain_first = norm_back(residual, inverse_first, gains_ref[0:1, :], grad_normed)
@@ -1270,28 +1311,23 @@
     swaps = [swap(0, pair)]
     swaps[0].start()
     grad_ref[...] = (grad_middle + through).T
-    own_y().wait()
-    for bits in (0, 2, 4, 6):
-        x_pair(bits).wait_send()
-        remote(
-            xf_all.at[:, tokens_of(p ^ bits ^ 1)], xf_all.at[:, tokens_of(p ^ bits ^ 1)],
-            ps.at[bits], pr.at[p ^ bits ^ 1], pair,
-        ).wait_recv()
+    @pl.when(p == 0)
+    def _():
+        own_y().start()
+        own_y().wait()
+        gradients(parts_late)
 
     @pl.when(p == 1)
     def _():
-        own_a().wait()
         own_v().wait()
-        for q in range(CLASSES):
-            if q != 1:
-                remote(xt_in.at[1], xa_all.at[:, tokens_of(q)], as_, ar.at[q], pair).wait_recv()
-                remote(dv_in, yv_all.at[tokens_of(q)], vs, vr.at[q], pair).wait_recv()
-
-    gradients()
+        value_gradient()
+
     swaps[0].wait()
     gain_s[1] = gain_s[0] + gain_r[0]
     swaps.append(swap(1, at.peer(2)))
     swaps[1].start()
+    for bits in (0, 2, 4, 6):
+        x_pair(bits).wait_send()
     for bits in range(1, CLASSES):
         y_move(bits).wait_send()
     for bits in (2, 4, 6):
@@ -1316,30 +1352,49 @@
 
     sall = wd.at[:, pl.ds(0, half)]
     ga, pa = (w01.at[1, pl.ds((parts - 1 - i) * rows, rows)] for i in range(2))
-    total = own[...]
-    for j in range(1, parts):
-        arrival(j).wait_recv()
-        total = total + za_r[j - 1].astype(F32)
-    ga[...] = total.astype(BF16)
-    sall[my_rows, :] = (MOMENTUM * ma[...] + total).astype(BF16)
-
-    def shard(index):
-        return sall.at[pl.ds(pl.multiple_of(index * rows, 16), rows)]
-
-    def rightward(index):
-        return remote(shard(index), shard(index), ls_r.at[index], lr_r.at[index], (at.c, lax.rem(f + 1, parts)))
-
-    def leftward(index):
-        return remote(shard(index), shard(index), ls_l.at[index], lr_l.at[index], (at.c, lax.rem(f + parts - 1, parts)))
-
-    def can_right():
-        return f < parts - 1
-
-    def can_left():
-        return f > 0
-
-    pl.when(can_right())(lambda: rightward(f).start())
-    pl.when(can_left())(lambda: leftward(f).start())
+
+    def shard(index, part):
+        return sall.at[pl.ds(pl.multiple_of(index * rows, 16), rows), part_lanes[part]]
+
+    def rightward(index, part):
+        here = shard(index, part)
+        return remote(here, here, ls_r.at[part, index], lr_r.at[part, index], (at.c, lax.rem(f + 1, parts)))
+
+    def leftward(index, part):
+        here = shard(index, part)
+        return remote(here, here, ls_l.at[part, index], lr_l.at[part, index], (at.c, lax.rem(f + parts - 1, parts)))
+
+    can_right = f < parts - 1
+    can_left = f > 0
+
+    def settle_part(part):
+        lanes = part_lanes[part]
+        total = own[:, lanes]
+        for j in range(1, parts):
+            arrival(j, part).wait_recv()
+            total = total + za_r[j - 1, :, lanes].astype(F32)
+        ga[:, lanes] = total.astype(BF16)
+        sall[my_rows, lanes] = (MOMENTUM * ma[:, lanes] + total).astype(BF16)
+        pl.when(can_right)(lambda: rightward(f, part).start())
+        pl.when(can_left)(lambda: leftward(f, part).start())
+
+    def hop_part(hop, part):
+        @pl.when(f - hop >= 0)
+        def _():
+            rightward(f - hop, part).wait_recv()
+            pl.when(can_right)(lambda: rightward(f - hop, part).start())
+
+        @pl.when(f + hop < parts)
+        def _():
+            leftward(f + hop, part).wait_recv()
+            pl.when(can_left)(lambda: leftward(f + hop, part).start())
+
+    for conditions in (parts_early, parts_late):
+        for part in range(2):
+            pl.when(conditions[part]())(lambda part=part: settle_part(part))
+        for hop in range(1, parts):
+            for part in range(2):
+                pl.when(conditions[part]())(lambda hop=hop, part=part: hop_part(hop, part))
 
     pass_on, finish = spread_even(at, ga, g_out, ag_l, ag_s, ag_r)
     swaps[2].wait()
@@ -1350,26 +1405,16 @@
     for copy in line_gain:
         copy.start()
 
-    for hop in range(1, parts):
-        @pl.when(f - hop >= 0)
-        def _(hop=hop):
-            rightward(f - hop).wait_recv()
-            pl.when(can_right())(lambda: rightward(f - hop).start())
-
-        @pl.when(f + hop < parts)
-        def _(hop=hop):
-            leftward(f + hop).wait_recv()
-            pl.when(can_left())(lambda: leftward(f + hop).start())
-
     pass_on()
 
-    for j in range(1, parts):
-        line(f ^ j, f).wait_send()
-    pl.when(can_right())(lambda: rightward(f).wait_send())
-    pl.when(can_left())(lambda: leftward(f).wait_send())
-    for hop in range(1, parts):
-        pl.when((f - hop >= 0) & can_right())(lambda hop=hop: rightward(f - hop).wait_send())
-        pl.when((f + hop < parts) & can_left())(lambda hop=hop: leftward(f + hop).wait_send())
+    for part in range(2):
+        for j in range(1, parts):
+            line(f ^ j, f, part).wait_send()
+        pl.when(can_right)(lambda: rightward(f, part).wait_send())
+        pl.when(can_left)(lambda: leftward(f, part).wait_send())
+        for hop in range(1, parts):
+            pl.when((f - hop >= 0) & can_right)(lambda hop=hop: rightward(f - hop, part).wait_send())
+            pl.when((f + hop < parts) & can_left)(lambda hop=hop: leftward(f + hop, part).wait_send())
     pl.semaphore_signal(free.at[1], inc=1, device_id=pair, device_id_type=MESH)
     pl.semaphore_wait(free.at[1], 1)
 
@@ -1621,10 +1666,10 @@
             dma((4, CLASSES, parts)), dma((7,)), dma((CLASSES,)), dma((3,)), dma((3,)),
             dma((4,)), dma((CLASSES,)), dma((CLASSES,)), dma((CLASSES,)), dma((CLASSES,)),
             dma((CLASSES,)), dma((CLASSES,)), dma, dma((CLASSES,)), dma, dma((CLASSES,)),
-            dma((2,)), dma((2,)), dma((parts,)), dma((parts,)),
+            dma((2,)), dma((2,)), dma((2, parts)), dma((2, parts)),
             dma((2,)), dma((n_gain,)), dma((n_gain,)),
             dma, dma((7,)), dma((CLASSES,)),
-            dma((parts,)), dma((parts,)), dma((parts,)), dma((parts,)),
+            dma((2, parts)), dma((2, parts)), dma((2, parts)), dma((2, parts)),
             dma((4,)), dma((2, 4)), dma, dma,
             dma((near,)), dma((near,)), dma, dma,
             dma, dma((7,)), dma((CLASSES,)), pltpu.SemaphoreType.REGULAR((2,)),

time: 398 us -> 391 us (0.982)
  the two profiles are of different devices: /device:TPU:3 before, /device:TPU:0 now
where the time goes in v1:
time: 391 us; the launch traced here: 383 us
  Pallas kernels  372 us (95%)
  local copies, waits for them, and re-layouts  5.42 us (1%)
  other arithmetic  4.81 us (1%)
    pallas_call x1, Pallas kernels, step_pass(): pl.pallas_call(step_kernel, out_shape=(jax.ShapeDtypeStruct((width, token...  352 us
    pallas_call x1, Pallas kernels, settle(): pl.pallas_call(functools.partial(settle_wide, (f_q, f_o, f_gate, f_up)),...  12.2 us

profile of v1, /device:TPU:0, one launch (start us, length us, event | category | flops | bytes accessed | tf_op | source)
XLA Modules:
  0.0 383.2 jit_solution(4811907695665707320)
XLA Ops:
  0.7 0.7 dynamic-slice_multiply_fusion
  1.4 0.1 iota_add_fusion.1
  1.5 0.1 add.79
  1.6 0.7 broadcast_multiply_fusion
  2.2 0.1 iota_add_fusion
  2.3 0.1 add.85
  2.4 1.0 fusion.2
  3.4 0.9 select_convert_fusion.bias_ref
  4.3 352.4 %step_pass.1 = (bf16[960,128]{1,0:T(8,128)(2,1)}, f32[960,128]{1,0:T(8,128)}, bf16[8,240,1280]{2,1,0:T(8,128)(2,1)}, bf16[8,240,1280]{2,1,0:T(8,128)(2,1)}, f32[8,960]{1,0:T(8,128)}) custom-call(bf16[960,128]{1,0:T(8,128)(2,1)} %bitcast.41, bf16[960,128]{1,0:T(8,128)(2,1)} %bitcast.42, f32[2,960]{1,0:T(2,128)} %gains_ref.1, ...), custom_call_target="tpu_custom_call" | custom-call | tf_op jit(solution)/shard_map/step_pass/pallas_call | solution.py:1623
  356.7 0.8 slice.3
  357.4 1.4 multiply_subtract_fusion
  358.8 0.0 copy-done.8
  358.8 0.0 copy-done.9
  358.8 0.0 copy-done.10
  358.8 0.0 copy-done.11
  358.8 0.0 copy-start
  358.8 1.7 copy-done
  360.5 1.3 copy-done.3
  361.8 0.0 copy-start.6
  361.8 0.0 copy-start.7
  361.8 7.3 %settle_turned.1 = (f32[960,640]{1,0:T(8,128)}, f32[960,640]{1,0:T(8,128)}, f32[960,640]{1,0:T(8,128)}, f32[320,240]{1,0:T(8,128)}, f32[320,240]{1,0:T(8,128)}, ...) custom-call(bf16[8,240,1280]{2,1,0:T(8,128)(2,1)} %get-tuple-element.54.refs_0_.g_tall.g_pair,, ...), custom_call_target="tpu_custom_call" | custom-call | tf_op jit(solution)/shard_map/settle_turned/pallas_call | solution.py:1757
  369.2 12.2 %settle_wide.1 = (f32[240,960]{1,0:T(8,128)}, f32[240,960]{1,0:T(8,128)}, f32[240,960]{1,0:T(8,128)}, f32[240,960]{1,0:T(8,128)}, f32[240,960]{1,0:T(8,128)}, /*...) custom-call(bf16[8,240,1280]{2,1,0:T(8,128)(2,1)} %get-tuple-element, ...), custom_call_target="tpu_custom_call" | custom-call | tf_op jit(solution)/shard_map/settle_wide/pallas_call | solution.py:1740
  381.4 0.7 copy.47
  382.1 0.8 copy.48
  (22 shorter events, 0.1 us)
Async XLA Ops:
  4.3 354.5 %copy-start.8 = (f32[240,320]{0,1:T(8,128)S(1)}, f32[240,320]{0,1:T(8,128)}, u32[]{:S(2)}) copy-start(f32[240,320]{0,1:T(8,128)} %param.30) | copy-start | bytes 921604
  4.3 354.5 %copy-start.9 = (f32[240,320]{0,1:T(8,128)S(1)}, f32[240,320]{0,1:T(8,128)}, u32[]{:S(2)}) copy-start(f32[240,320]{0,1:T(8,128)} %param.31) | copy-start | bytes 921604
  4.3 354.5 %copy-start.10 = (bf16[240,320]{0,1:T(8,128)(2,1)S(1)}, bf16[240,320]{0,1:T(8,128)(2,1)}, u32[]{:S(2)}) copy-start(bf16[240,320]{0,1:T(8,128)(2,1)} %param.22) | copy-start | bytes 460804
  4.3 354.5 %copy-start.11 = (bf16[240,320]{0,1:T(8,128)(2,1)S(1)}, bf16[240,320]{0,1:T(8,128)(2,1)}, u32[]{:S(2)}) copy-start(bf16[240,320]{0,1:T(8,128)(2,1)} %param.23) | copy-start | bytes 460804
  358.8 1.7 copy-start
  360.5 1.3 copy-start.3
  361.8 7.4 %copy-start.1 = (bf16[240,2560]{1,0:T(8,128)(2,1)S(1)}, bf16[240,2560]{1,0:T(8,128)(2,1)}, u32[]{:S(2)}) copy-start(bf16[240,2560]{1,0:T(8,128)(2,1)} %refs_8_.1) | copy-start | bytes 3686404
  361.8 7.4 %copy-start.2 = (bf16[240,2560]{1,0:T(8,128)(2,1)S(1)}, bf16[240,2560]{1,0:T(8,128)(2,1)}, u32[]{:S(2)}) copy-start(bf16[240,2560]{1,0:T(8,128)(2,1)} %refs_9_.1) | copy-start | bytes 3686404
  361.8 7.4 %copy-start.4 = (f32[240,960]{1,0:T(8,128)S(1)}, f32[240,960]{1,0:T(8,128)}, u32[]{:S(2)}) copy-start(f32[240,960]{1,0:T(8,128)} %refs_2_.1) | copy-start | bytes 2764804
  361.8 7.4 %copy-start.5 = (f32[240,960]{1,0:T(8,128)S(1)}, f32[240,960]{1,0:T(8,128)}, u32[]{:S(2)}) copy-start(f32[240,960]{1,0:T(8,128)} %refs_3_.1) | copy-start | bytes 2764804
  361.8 7.4 %copy-start.6 = (bf16[240,960]{1,0:T(8,128)(2,1)S(1)}, bf16[240,960]{1,0:T(8,128)(2,1)}, u32[]{:S(2)}) copy-start(bf16[240,960]{1,0:T(8,128)(2,1)} %refs_6_.1) | copy-start | bytes 1382404
  361.8 7.4 %copy-start.7 = (bf16[240,960]{1,0:T(8,128)(2,1)S(1)}, bf16[240,960]{1,0:T(8,128)(2,1)}, u32[]{:S(2)}) copy-start(bf16[240,960]{1,0:T(8,128)(2,1)} %refs_7_.1) | copy-start | bytes 1382404
  369.2 12.2 %copy-start.13 = (bf16[960,128]{1,0:T(8,128)(2,1)S(1)}, bf16[960,128]{1,0:T(8,128)(2,1)}, u32[]{:S(2)}) copy-start(bf16[960,128]{1,0:T(8,128)(2,1)} %get-tuple-element.52) | copy-start | bytes 737284
  369.2 12.9 %copy-start.12 = (f32[960,128]{1,0:T(8,128)S(1)}, f32[960,128]{1,0:T(8,128)}, u32[]{:S(2)}) copy-start(f32[960,128]{1,0:T(8,128)} %get-tuple-element.53) | copy-start | bytes 1474564
